TPU v7x, 32 devices: a whole 2x2x4 slice. The times are simulated.
32 devices in a mesh: member: 2 (over y), band: 4 (over z), fld: 2 (over x), sub: 2 (over core).
Axes of the slice: x: 2, y: 2, z: 4, core: 2. Of those that a mesh axis runs over, the one named last changes fastest.
Arguments:
- spectra: bfloat16 [8, 16, 3, 2, 1280], P(('member', 'band'), ('fld', 'sub')), parts along dimension 0, may hold values from -2 to 2
- legendre: bfloat16 [4, 1280, 1280], P('band'), may hold values from -0.15625 to 0.15625
- assignment: int32 [4], replicated, may hold values from 0 to 3, each once
- circle_longitudes: int32 [1280], replicated, may hold values from 12 to 5136, as said below
- coriolis: float32 [2, 1280], replicated, may hold values from -1.5 to 1.5
- weights: float32 [2, 1280], replicated, may hold values from 13 to 138
- thickness: float32 [16], P(('fld', 'sub')), may hold values from 0.5 to 5
Outputs:
- tendencies: bfloat16 [8, 16, 3, 2, 1280], P(('member', 'band'), ('fld', 'sub')), parts along dimension 0
There are 2 independent parts, one for each index of `member`. A program takes and returns all parts, laid end to end along the dimension named above; an argument that names none is the same for every part. Nothing has to cross between parts.
Inputs may be any that keep to these rules, and one draw needn't show every extreme that they name: Each value once: slot s holds the wavenumber 320 * assignment[s]. `circle_longitudes`: row h of each hemisphere (h counted from the pole) holds between 12 + 4 h and 20 + 4 h points, a multiple of four, the same in both hemispheres; row 1279 holds 5136.
All inputs are finite; a program needn't handle non-finite values.
Results may differ from a plain program's by a relative error of at most 0.0059.
Values may be sent and summed in bfloat16 or wider, within the bound.
A program may use at most 128 MiB of HBM per device.

v0:
```python
import jax
import jax.numpy as jnp
from jax import lax
from jax.sharding import PartitionSpec as P

TWO_PI = 6.283185307179586


def carried_in(value, axis, join, neutral):
    count, mine = (lax.axis_size(axis), lax.axis_index(axis))
    pieces = lax.all_gather(value, axis)
    pieces = pieces[::-1]
    mine = count - 1 - mine
    subtotal = jnp.full_like(value, 0) + jnp.asarray(neutral, value.dtype)

    def hop(position, subtotal):
        longer = join(subtotal, pieces[position])
        return jnp.where(position < mine, longer, subtotal)

    return lax.fori_loop(0, count - 1, hop, subtotal)


def wave_masks(wavenumbers, coeff_count):
    row_index = jnp.arange(coeff_count, dtype=jnp.int32)
    inside = row_index[None, :] < (coeff_count - wavenumbers)[:, None]
    part_index = jnp.arange(2, dtype=jnp.int32)
    real_ok = (part_index[None, :] == 0) | (wavenumbers[:, None] > 0)
    return inside[:, None, :] & real_ok[:, :, None]


def trig_tables(wavenumbers, counts, row_bound):
    positions = jnp.arange(row_bound, dtype=jnp.int32)
    phase_index = wavenumbers[None, :, None] * positions[None, None, :] % counts[:, None, None]
    angles = TWO_PI * phase_index.astype(jnp.float32) / counts[:, None, None].astype(jnp.float32)
    inside_row = positions[None, None, :] < counts[:, None, None]
    cosine = jnp.where(inside_row, jnp.cos(angles), 0.0)
    sine_part = jnp.where(inside_row, jnp.sin(angles), 0.0)
    return jnp.stack([cosine, sine_part], axis=1).astype(jnp.bfloat16)


def inverse_factor(wavenumbers, counts):
    resolved = 2 * wavenumbers[None, :] < counts[:, None]
    gain_value = jnp.where(resolved, jnp.where(wavenumbers[None, :] == 0, 1.0, 2.0), 0.0)
    sign_pair = jnp.array([1.0, -1.0], dtype=jnp.float32)
    return gain_value[:, None, :] * sign_pair[None, :, None]


def direct_scale(wavenumbers, counts, quadrature):
    resolved = 2 * wavenumbers[None, :] < counts[:, None]
    unit_multiplier = jnp.where(resolved, 1.0, 0.0) / counts[:, None].astype(jnp.float32)
    sign_pair = jnp.array([1.0, -1.0], dtype=jnp.float32)
    return (
        quadrature[:, :, None, None]
        * sign_pair[None, None, :, None]
        * unit_multiplier[:, None, None, :]
    )


def tendency_terms(physical_samples, planetary):
    vorticity = physical_samples[:, :, :, 0]
    spreading_rate_grid = physical_samples[:, :, :, 1]
    thermal_state = physical_samples[:, :, :, 2]
    absolute = vorticity + planetary[:, :, None, None]
    return jnp.stack(
        [
            -absolute * spreading_rate_grid,
            absolute * vorticity,
            0.5 * (vorticity * vorticity + spreading_rate_grid * spreading_rate_grid),
            -thermal_state * spreading_rate_grid,
        ],
        axis=3,
    ).astype(jnp.bfloat16)


def add_terms(earlier_sum, later_sum):
    return earlier_sum + later_sum


def on_device(spectra, legendre, assignment, circle_longitudes, coriolis, weights, thickness):
    waves_dev = spectra.shape[0]
    layers_per_chip = spectra.shape[1]
    coeff_count = spectra.shape[4]
    lat_half = legendre.shape[2]
    band_count = lax.axis_size("band")
    band_place = lax.axis_index("band")
    wave_total = waves_dev * band_count
    stride_size = coeff_count // wave_total
    all_waves = stride_size * assignment
    own_waves = lax.dynamic_slice_in_dim(all_waves, band_place * waves_dev, waves_dev)
    keeper = wave_masks(own_waves, coeff_count)
    masked = jnp.where(keeper[:, None, None, :, :], spectra, jnp.zeros_like(spectra))
    parity = jnp.where(jnp.arange(coeff_count) % 2 == 0, 1.0, -1.0).astype(jnp.float32)
    flipped = masked * parity.astype(jnp.bfloat16)[None, None, None, None, :]
    stacked = jnp.stack([masked, flipped], axis=1)
    both_sides = jnp.einsum(
        "ktp,kelfrt->kelfrp", legendre, stacked, preferred_element_type=jnp.float32
    )
    north_part = both_sides[:, 0]
    austral_portion = both_sides[:, 1]
    fourier = jnp.stack([north_part, austral_portion], axis=1).astype(jnp.bfloat16)
    slot_count = lat_half // band_count
    outgoing = fourier.reshape(waves_dev, 2, layers_per_chip, 3, 2, slot_count, band_count)
    arrived = lax.all_to_all(outgoing, "band", split_axis=6, concat_axis=0, tiled=True)
    gridded = arrived.reshape(wave_total, 2, layers_per_chip, 3, 2, slot_count)
    own_counts = lax.dynamic_slice_in_dim(
        circle_longitudes.reshape(slot_count, band_count), band_place, 1, axis=1
    )[:, 0]
    own_planet = jnp.transpose(
        lax.dynamic_slice_in_dim(
            coriolis.reshape(2, slot_count, band_count), band_place, 1, axis=2
        )[:, :, 0]
    )
    own_quad = jnp.transpose(
        lax.dynamic_slice_in_dim(weights.reshape(2, slot_count, band_count), band_place, 1, axis=2)[
            :, :, 0
        ]
    )
    block_count = max(
        (divisor for divisor in range(1, min(8, slot_count) + 1) if slot_count % divisor == 0)
    )
    tile_extent = slot_count // block_count
    pieces = []
    for block_index in range(block_count):
        first_slot = block_index * tile_extent
        last_slot = first_slot + tile_extent - 1
        row_bound = 20 + 4 * (band_count * last_slot + band_count - 1)
        row_bound = -(-row_bound // 128) * 128
        counts = own_counts[first_slot : first_slot + tile_extent]
        tables = trig_tables(all_waves, counts, row_bound)
        gain_lookup = jnp.transpose(inverse_factor(all_waves, counts), (2, 1, 0)).astype(
            jnp.bfloat16
        )
        coeff_block = (
            gridded[..., first_slot : first_slot + tile_extent]
            * gain_lookup[:, None, None, None, :, :]
        )
        physical_samples = jnp.einsum(
            "kelfrj,jrkx->jelfx", coeff_block, tables, preferred_element_type=jnp.float32
        )
        tendency = tendency_terms(
            physical_samples, own_planet[first_slot : first_slot + tile_extent]
        )
        summed = jnp.einsum(
            "jelqx,jrkx->kelqrj", tendency, tables, preferred_element_type=jnp.float32
        )
        factor = jnp.transpose(
            direct_scale(all_waves, counts, own_quad[first_slot : first_slot + tile_extent]),
            (3, 1, 2, 0),
        )
        pieces.append((summed * factor[:, :, None, None, :, :]).astype(jnp.bfloat16))
    returned = jnp.concatenate(pieces, axis=5)
    outward = returned.reshape(wave_total, 2, layers_per_chip, 4, 2, slot_count, 1)
    landed = lax.all_to_all(outward, "band", split_axis=0, concat_axis=6, tiled=True)
    spectral_back = landed.reshape(waves_dev, 2, layers_per_chip, 4, 2, lat_half)
    projected = jnp.einsum(
        "ktp,kelqrp->kelqrt", legendre, spectral_back, preferred_element_type=jnp.float32
    )
    combined = projected[:, 0] + parity * projected[:, 1]
    weighted = masked[:, :, 2].astype(jnp.float32) * thickness[None, :, None, None]
    column_local = jnp.cumsum(weighted[:, ::-1], axis=1)[:, ::-1]
    below_sum = carried_in(
        jnp.sum(weighted, axis=1),
        ("fld", "sub"),
        add_terms,
        jnp.zeros((waves_dev, 2, coeff_count), jnp.float32),
    )
    column = column_local + below_sum[:, None]
    degree = own_waves[:, None] + jnp.arange(coeff_count, dtype=jnp.int32)[None, :]
    truncation_value = coeff_count - 1
    laplace = (degree * (degree + 1)).astype(jnp.float32) / float(
        truncation_value * (truncation_value + 1)
    )
    divergence_tend = combined[:, :, 1] + laplace[:, None, None, :] * (column + combined[:, :, 2])
    result = jnp.stack([combined[:, :, 0], divergence_tend, combined[:, :, 3]], axis=2)
    result = jnp.where(keeper[:, None, None, :, :], result, 0.0)
    return result.astype(jnp.bfloat16)


def solution(mesh):
    in_specs = (
        P(("member", "band"), ("fld", "sub"), None, None, None),
        P("band", None, None),
        P(),
        P(),
        P(),
        P(),
        P(("fld", "sub")),
    )
    out_specs = P(("member", "band"), ("fld", "sub"), None, None, None)
    return jax.shard_map(
        on_device, mesh=mesh, in_specs=in_specs, out_specs=out_specs, check_vma=False
    )
```

profile of v0, /device:TPU:0, one launch (start us, length us, event | category | flops | bytes accessed | tf_op | source)
XLA Modules:
  0.0 1077.8 jit_solution(9537342005354708111)
XLA Ops:
  5.4 9.5 reshape.1922
  14.9 4.4 copy.107
  19.3 6.3 all-to-all-start
  26.5 1.8 convert_reduce_fusion
  57.7 1.8 reshape.1888
  59.5 1.8 reshape.1887
  81.6 2.0 fusion.232
  83.7 5.7 all-gather.1
  103.1 15.8 %select_convert_fusion.15 = (bf16[40,1,4,768]{3,2,1,0:T(4,128)(2,1)}, bf16[40,1,4,768]{3,2,1,0:T(4,128)(2,1)}) fusion(f32[40]{0:T(128)} %get-tuple-element.262, pred[40]{0:T(512)(128)(4,1)} %get-tuple-element.271, s32[40]{0:T(128)} %get-tuple-element.263, s32[4,768]{1,0:T(4,128)} %iota_multiply_fusion.7, pred[40,768]{1,0:T(8,128)(4,1)} %iota_compare_fusion.7), kind=kLoop, calls=%fused_computation.240 | loop fusion | flops 1720320 | bytes 534888 | tf_op jit(solution)/shard_map/convert.47
  118.9 26.6 %select_convert_fusion.13 = (bf16[40,1,4,1408]{3,2,1,0:T(4,128)(2,1)}, bf16[40,1,4,1408]{3,2,1,0:T(4,128)(2,1)}) fusion(f32[40]{0:T(128)} %get-tuple-element.251, pred[40]{0:T(512)(128)(4,1)} %get-tuple-element.270, s32[40]{0:T(128)} %get-tuple-element.250, s32[4,1408]{1,0:T(4,128)} %iota_multiply_fusion.6, pred[40,1408]{1,0:T(8,128)(4,1)} %iota_compare_fusion.6), kind=kLoop, calls=%fused_computation.226 | loop fusion | flops 3153920 | bytes 980328 | tf_op jit(solution)/shard_map/convert.41
  145.5 37.4 %select_convert_fusion.11 = (bf16[40,1,4,2048]{3,2,1,0:T(4,128)(2,1)}, bf16[40,1,4,2048]{3,2,1,0:T(4,128)(2,1)}) fusion(f32[40]{0:T(128)} %get-tuple-element.260, pred[40]{0:T(512)(128)(4,1)} %get-tuple-element.269, s32[40]{0:T(128)} %get-tuple-element.261, s32[4,2048]{1,0:T(4,128)} %iota_multiply_fusion.5, pred[40,2048]{1,0:T(8,128)(4,1)} %iota_compare_fusion.5), kind=kLoop, calls=%fused_computation.205 | loop fusion | flops 4587520 | bytes 1425768 | tf_op jit(solution)/shard_map/convert.35
  182.9 48.4 %select_convert_fusion.9 = (bf16[40,1,4,2688]{3,2,1,0:T(4,128)(2,1)}, bf16[40,1,4,2688]{3,2,1,0:T(4,128)(2,1)}) fusion(f32[40]{0:T(128)} %get-tuple-element.247, pred[40]{0:T(512)(128)(4,1)} %get-tuple-element.268, s32[40]{0:T(128)} %get-tuple-element.246, s32[4,2688]{1,0:T(4,128)S(1)} %copy-done.35, pred[40,2688]{1,0:T(8,128)(4,1)S(1)} %iota_compare_fusion.4), kind=kLoop, calls=%fused_computation.177 | loop fusion | flops 6021120 | bytes 1871208 | tf_op jit(solution)/shard_map/convert.29
  231.4 58.9 %select_convert_fusion.7 = (bf16[40,1,4,3328]{3,2,1,0:T(4,128)(2,1)}, bf16[40,1,4,3328]{3,2,1,0:T(4,128)(2,1)}) fusion(f32[40]{0:T(128)} %get-tuple-element.258, pred[40]{0:T(512)(128)(4,1)} %get-tuple-element.267, s32[40]{0:T(128)} %get-tuple-element.259, s32[4,3328]{1,0:T(4,128)S(1)} %copy-done.29, pred[40,3328]{1,0:T(8,128)(4,1)S(1)} %copy-done.19), kind=kLoop, calls=%fused_computation.152 | loop fusion | flops 7454720 | bytes 2316648 | tf_op jit(solution)/shard_map/convert.23
  290.4 68.9 %select_convert_fusion.5 = (bf16[40,1,4,3968]{3,2,1,0:T(4,128)(2,1)}, bf16[40,1,4,3968]{3,2,1,0:T(4,128)(2,1)}) fusion(f32[40]{0:T(128)S(1)} %copy-done.74, pred[40]{0:T(512)(128)(4,1)S(1)} %copy-done.75, s32[40]{0:T(128)S(1)} %copy-done.73, s32[4,3968]{1,0:T(4,128)S(1)} %copy-done.28, pred[40,3968]{1,0:T(8,128)(4,1)S(1)} %copy-done.18), kind=kLoop, calls=%fused_computation.138 | loop fusion | flops 8888320 | bytes 2762088 | tf_op jit(solution)/shard_map/convert.17
  359.4 79.9 %select_convert_fusion.3 = (bf16[40,1,4,4608]{3,2,1,0:T(4,128)(2,1)}, bf16[40,1,4,4608]{3,2,1,0:T(4,128)(2,1)}) fusion(f32[40]{0:T(128)S(1)} %copy-done.70, pred[40]{0:T(512)(128)(4,1)S(1)} %copy-done.72, s32[40]{0:T(128)S(1)} %copy-done.71, s32[4,4608]{1,0:T(4,128)S(1)} %copy-done.23, pred[40,4608]{1,0:T(8,128)(4,1)S(1)} %copy-done.17), kind=kLoop, calls=%fused_computation.117 | loop fusion | flops 10321920 | bytes 3207528 | tf_op jit(solution)/shard_map/convert.11
  439.3 91.1 %select_convert_fusion.1 = (bf16[40,1,4,5248]{3,2,1,0:T(4,128)(2,1)}, bf16[40,1,4,5248]{3,2,1,0:T(4,128)(2,1)}) fusion(f32[40]{0:T(128)S(1)} %copy-done.77, pred[40]{0:T(512)(128)(4,1)S(1)} %copy-done.78, s32[40]{0:T(128)S(1)} %copy-done.76, s32[4,5248]{1,0:T(4,128)S(1)} %copy-done.21, pred[40,5248]{1,0:T(8,128)(4,1)S(1)} %copy-done.16), kind=kLoop, calls=%fused_computation.103 | loop fusion | flops 11755520 | bytes 3652968 | tf_op jit(solution)/shard_map/convert.5
  531.2 1.7 slice_multiply_fusion
  532.8 2.1 copy.109
  534.9 2.5 convolution_bitcast_fusion.7
  537.4 1.8 fusion.172
  540.7 10.2 fusion.156
  550.9 2.6 copy.113
  554.8 3.4 convolution_bitcast_fusion.6
  558.2 2.2 fusion.85
  560.5 2.8 maximum_bitcast_fusion.6
  563.3 19.4 %fusion.153 = bf16[4,2,4,4,2,40]{3,0,2,1,4,5:T(4,128)(2,1)} fusion(bf16[40,2,4,4,1408,1]{4,2,3,1,0,5:T(4,128)(2,1)S(1)} %maximum_bitcast_fusion.6, f32[4,2,2,40]{0,1,2,3:T(2,128)S(1)} %copy-done.48, bf16[40,1,4,1408]{3,2,1,0:T(4,128)(2,1)S(1)} %copy-done.13, bf16[40,1,4,1408]{3,2,1,0:T(4,128)(2,1)S(1)} %copy-done.12), kind=kOutput, calls=%fused_computation.195 | convolution fusion | flops 30658560 | bytes 4528640 | tf_op jit(solution)/shard_map/jelqx,jrkx->kelqrj/dot_general | solution.py:143
  582.6 2.6 copy.119
  586.5 4.3 convolution_bitcast_fusion.5
  590.8 3.3 fusion.58
  594.1 4.1 maximum_bitcast_fusion.5
  598.3 25.7 %fusion.150 = bf16[4,2,4,4,2,40]{3,0,2,1,4,5:T(4,128)(2,1)} fusion(bf16[40,2,4,4,2048,1]{4,2,3,1,0,5:T(4,128)(2,1)S(1)} %maximum_bitcast_fusion.5, f32[4,2,2,40]{0,1,2,3:T(2,128)S(1)} %copy-done.47, bf16[40,1,4,2048]{3,2,1,0:T(4,128)(2,1)S(1)} %copy-done.11, bf16[40,1,4,2048]{3,2,1,0:T(4,128)(2,1)S(1)} %copy-done.10), kind=kOutput, calls=%fused_computation.194 | convolution fusion | flops 44584960 | bytes 6576640 | tf_op jit(solution)/shard_map/jelqx,jrkx->kelqrj/dot_general | solution.py:143
  624.0 2.6 copy.125
  627.9 5.4 convolution_bitcast_fusion.4
  633.3 3.4 fusion.35
  636.7 5.3 maximum_bitcast_fusion.4
  642.1 36.8 %fusion.145 = bf16[4,2,4,4,2,40]{3,0,2,1,4,5:T(4,128)(2,1)} fusion(bf16[40,2,4,4,2688,1]{4,2,3,1,0,5:T(4,128)(2,1)S(1)} %maximum_bitcast_fusion.4, f32[4,2,2,40]{0,1,2,3:T(2,128)S(1)} %copy-done.46, bf16[40,1,4,2688]{3,2,1,0:T(4,128)(2,1)} %get-tuple-element.173, bf16[40,1,4,2688]{3,2,1,0:T(4,128)(2,1)S(1)} %copy-done.9), kind=kOutput, calls=%fused_computation.193 | convolution fusion | flops 58511360 | bytes 8624640 | tf_op jit(solution)/shard_map/jelqx,jrkx->kelqrj/dot_general | solution.py:143
  678.9 2.6 copy.131
  682.8 10.8 %convolution_bitcast_fusion.3 = f32[40,2,4,3,3328]{4,2,3,1,0:T(4,128)} fusion(bf16[4,2,4,3,2,40]{0,2,4,3,1,5:T(4,128)(2,1)} %copy.133, bf16[40,1,4,3328]{3,2,1,0:T(4,128)(2,1)} %get-tuple-element.169, bf16[40,1,4,3328]{3,2,1,0:T(4,128)(2,1)} %get-tuple-element.168), kind=kOutput, calls=%fused_computation.18 | convolution fusion | flops 55377920 | bytes 14924800 | tf_op jit(solution)/shard_map/kelfrj,jrkx->jelfx/dot_general | solution.py:137
  693.6 6.9 fusion.28
  700.5 6.9 maximum_bitcast_fusion.3
  707.5 41.9 %fusion.140 = bf16[4,2,4,4,2,40]{3,0,2,1,4,5:T(4,128)(2,1)} fusion(bf16[40,2,4,4,3328,1]{4,2,3,1,0,5:T(4,128)(2,1)S(1)} %maximum_bitcast_fusion.3, f32[4,2,2,40]{0,1,2,3:T(2,128)S(1)} %copy-done.45, bf16[40,1,4,3328]{3,2,1,0:T(4,128)(2,1)S(1)} %copy-done.8, bf16[40,1,4,3328]{3,2,1,0:T(4,128)(2,1)S(1)} %copy-done.7), kind=kOutput, calls=%fused_computation.192 | convolution fusion | flops 72437760 | bytes 10672640 | tf_op jit(solution)/shard_map/jelqx,jrkx->kelqrj/dot_general | solution.py:143
  749.4 2.6 copy.137
  753.3 12.6 %convolution_bitcast_fusion.2 = f32[40,2,4,3,3968]{4,2,3,1,0:T(4,128)} fusion(bf16[4,2,4,3,2,40]{0,2,4,3,1,5:T(4,128)(2,1)} %copy.139, bf16[40,1,4,3968]{3,2,1,0:T(4,128)(2,1)} %get-tuple-element.167, bf16[40,1,4,3968]{3,2,1,0:T(4,128)(2,1)} %get-tuple-element.166), kind=kOutput, calls=%fused_computation.17 | convolution fusion | flops 66027520 | bytes 17792000 | tf_op jit(solution)/shard_map/kelfrj,jrkx->jelfx/dot_general | solution.py:137
  765.9 8.2 fusion.23
  774.1 8.5 maximum_bitcast_fusion.2
  782.6 51.5 %fusion.159 = bf16[4,2,4,4,2,40]{3,0,2,1,4,5:T(4,128)(2,1)} fusion(bf16[40,2,4,4,3968,1]{4,2,3,1,0,5:T(4,128)(2,1)S(1)} %maximum_bitcast_fusion.2, bf16[40,1,4,3968]{3,2,1,0:T(4,128)(2,1)S(1)} %copy-done.6, bf16[40,1,4,3968]{3,2,1,0:T(4,128)(2,1)S(1)} %copy-done.5, f32[4,2,2,40]{0,1,2,3:T(2,128)S(1)} %copy-done.44), kind=kOutput, calls=%fused_computation.197 | convolution fusion | flops 86364160 | bytes 12720640 | tf_op jit(solution)/shard_map/jelqx,jrkx->kelqrj/dot_general | solution.py:143
  834.1 2.6 copy.143
  838.0 11.3 %convolution_bitcast_fusion.1 = f32[40,2,4,3,4608]{4,2,3,1,0:T(4,128)} fusion(bf16[4,2,4,3,2,40]{0,2,4,3,1,5:T(4,128)(2,1)} %copy.145, bf16[40,1,4,4608]{3,2,1,0:T(4,128)(2,1)} %get-tuple-element.165, bf16[40,1,4,4608]{3,2,1,0:T(4,128)(2,1)} %get-tuple-element.164), kind=kOutput, calls=%fused_computation.8 | convolution fusion | flops 76677120 | bytes 20659200 | tf_op jit(solution)/shard_map/kelfrj,jrkx->jelfx/dot_general | solution.py:137
  849.3 9.7 fusion.16
  859.1 10.0 maximum_bitcast_fusion.1
  869.1 60.9 %fusion.135 = bf16[4,2,4,4,2,40]{3,0,2,1,4,5:T(4,128)(2,1)} fusion(bf16[40,2,4,4,4608,1]{4,2,3,1,0,5:T(4,128)(2,1)} %maximum_bitcast_fusion.1, bf16[40,1,4,4608]{3,2,1,0:T(4,128)(2,1)S(1)} %copy-done.4, bf16[40,1,4,4608]{3,2,1,0:T(4,128)(2,1)S(1)} %copy-done.3, f32[4,2,2,40]{0,1,2,3:T(2,128)S(1)} %copy-done.43), kind=kOutput, calls=%fused_computation.189 | convolution fusion | flops 100290560 | bytes 14768640 | tf_op jit(solution)/shard_map/jelqx,jrkx->kelqrj/dot_general | solution.py:143
  930.0 2.6 copy.149
  933.9 12.9 %convolution_bitcast_fusion = f32[40,2,4,3,5248]{4,2,3,1,0:T(4,128)} fusion(bf16[4,2,4,3,2,40]{0,2,4,3,1,5:T(4,128)(2,1)} %copy.151, bf16[40,1,4,5248]{3,2,1,0:T(4,128)(2,1)} %get-tuple-element.163, bf16[40,1,4,5248]{3,2,1,0:T(4,128)(2,1)} %get-tuple-element.162), kind=kOutput, calls=%fused_computation.4 | convolution fusion | flops 87326720 | bytes 23526400 | tf_op jit(solution)/shard_map/kelfrj,jrkx->jelfx/dot_general | solution.py:137
  946.8 9.8 fusion.11
  956.6 13.3 %maximum_bitcast_fusion = bf16[40,2,4,4,5248,1]{4,2,3,1,0,5:T(4,128)(2,1)} fusion(bf16[40,2,4,1,5248]{4,2,3,1,0:T(4,128)(2,1)S(1)} %get-tuple-element.133, bf16[40,2,4,1,5248]{4,2,3,1,0:T(4,128)(2,1)S(1)} %get-tuple-element.132, bf16[40,2,4,1,5248]{4,2,3,1,0:T(4,128)(2,1)S(1)} %get-tuple-element.131, bf16[40,2,4,1,5248]{4,2,3,1,0:T(4,128)(2,1)S(1)} %get-tuple-element.130), kind=kLoop, calls=%fused_computation.1 | loop fusion | flops 20152320 | bytes 26869760 | tf_op jit(solution)/shard_map/stack | solution.py:64
  969.9 70.2 %fusion.130 = bf16[4,2,4,4,2,40]{3,0,2,1,4,5:T(4,128)(2,1)} fusion(bf16[40,2,4,4,5248,1]{4,2,3,1,0,5:T(4,128)(2,1)} %maximum_bitcast_fusion, bf16[40,1,4,5248]{3,2,1,0:T(4,128)(2,1)S(1)} %copy-done.2, bf16[40,1,4,5248]{3,2,1,0:T(4,128)(2,1)S(1)} %copy-done.1, f32[4,2,2,40]{0,1,2,3:T(2,128)S(1)} %copy-done.42), kind=kOutput, calls=%fused_computation.188 | convolution fusion | flops 114216960 | bytes 16816640 | tf_op jit(solution)/shard_map/jelqx,jrkx->kelqrj/dot_general | solution.py:143
  1040.2 2.6 copy.155
  1042.8 2.2 concatenate.11
  1045.0 5.1 all-to-all-start.1
  1050.1 2.2 while.14
  1052.3 3.5 rev.9
  1056.6 3.6 rev.10
  1060.7 3.7 copy.215
  1064.5 11.1 %reshape.1924 = bf16[2,4,4,2,1280]{4,1,3,2,0:T(4,128)(2,1)S(1)} reshape(bf16[1,2,4,4,2,320,4,1]{6,5,2,4,3,1,7,0:T(8,128)(2,1)} %copy.215) | data formatting | bytes 327680 | tf_op jit(solution)/shard_map/reshape.91
  (257 shorter events, 85.2 us)
Async XLA Ops:
  14.9 10.7 copy-start.68
  14.9 14.5 %copy-start.79 = (s32[4]{0:T(128)S(1)}, s32[4]{0:T(128)}, u32[]{:S(2)}) copy-start(s32[4]{0:T(128)} %param.27) | copy-start | bytes 52
  19.3 511.9 %all-to-all-start = ((bf16[1,2,4,3,2,320,4]{5,2,4,3,1,0,6:T(4,128)(2,1)}), bf16[1,2,4,3,2,320,4]{5,2,4,3,1,0,6:T(4,128)(2,1)S(1)}, u32[]{:S(2)}, u32[]{:S(2)}) async-start(bf16[1,2,4,3,2,320,4]{5,2,4,3,1,0,6:T(4,128)(2,1)} %copy.107), calls=%async_computation | async-start | bytes 294912 | tf_op jit(solution)/shard_map/all_to_all | solution.py:103
  29.4 7.1 copy-start.57
  29.4 7.1 copy-start.58
  29.4 7.1 copy-start.59
  29.4 15.5 %copy-start.52 = (s32[40]{0:T(128)}, s32[40]{0:T(128)S(1)}, u32[]{:S(2)}) copy-start(s32[40]{0:T(128)S(1)} %get-tuple-element.112) | copy-start | bytes 484
  29.4 15.5 %copy-start.53 = (s32[40]{0:T(128)}, s32[40]{0:T(128)S(1)}, u32[]{:S(2)}) copy-start(s32[40]{0:T(128)S(1)} %get-tuple-element.113) | copy-start | bytes 484
  29.5 15.5 %copy-start.54 = (s32[40]{0:T(128)}, s32[40]{0:T(128)S(1)}, u32[]{:S(2)}) copy-start(s32[40]{0:T(128)S(1)} %get-tuple-element.114) | copy-start | bytes 484
  29.5 15.5 %copy-start.55 = (s32[40]{0:T(128)}, s32[40]{0:T(128)S(1)}, u32[]{:S(2)}) copy-start(s32[40]{0:T(128)S(1)} %get-tuple-element.115) | copy-start | bytes 484
  29.5 15.5 %copy-start.56 = (s32[40]{0:T(128)}, s32[40]{0:T(128)S(1)}, u32[]{:S(2)}) copy-start(s32[40]{0:T(128)S(1)} %get-tuple-element.116) | copy-start | bytes 484
  103.1 79.8 %copy-start.35 = (s32[4,2688]{1,0:T(4,128)S(1)}, s32[4,2688]{1,0:T(4,128)}, u32[]{:S(2)}) copy-start(s32[4,2688]{1,0:T(4,128)} %iota_multiply_fusion.4) | copy-start | bytes 129028
  103.1 128.3 %copy-start.19 = (pred[40,3328]{1,0:T(8,128)(4,1)S(1)}, pred[40,3328]{1,0:T(8,128)(4,1)}, u32[]{:S(2)}) copy-start(pred[40,3328]{1,0:T(8,128)(4,1)} %iota_compare_fusion.3) | copy-start | bytes 399364
  103.1 128.3 %copy-start.29 = (s32[4,3328]{1,0:T(4,128)S(1)}, s32[4,3328]{1,0:T(4,128)}, u32[]{:S(2)}) copy-start(s32[4,3328]{1,0:T(4,128)} %iota_multiply_fusion.3) | copy-start | bytes 159748
  145.4 144.8 %copy-start.18 = (pred[40,3968]{1,0:T(8,128)(4,1)S(1)}, pred[40,3968]{1,0:T(8,128)(4,1)}, u32[]{:S(2)}) copy-start(pred[40,3968]{1,0:T(8,128)(4,1)} %iota_compare_fusion.2) | copy-start | bytes 476164
  145.4 144.9 %copy-start.28 = (s32[4,3968]{1,0:T(4,128)S(1)}, s32[4,3968]{1,0:T(4,128)}, u32[]{:S(2)}) copy-start(s32[4,3968]{1,0:T(4,128)} %iota_multiply_fusion.2) | copy-start | bytes 190468
  145.4 144.9 %copy-start.73 = (s32[40]{0:T(128)S(1)}, s32[40]{0:T(128)}, u32[]{:S(2)}) copy-start(s32[40]{0:T(128)} %get-tuple-element.242) | copy-start | bytes 484
  145.5 144.9 %copy-start.74 = (f32[40]{0:T(128)S(1)}, f32[40]{0:T(128)}, u32[]{:S(2)}) copy-start(f32[40]{0:T(128)} %get-tuple-element.243) | copy-start | bytes 484
  145.5 144.9 %copy-start.75 = (pred[40]{0:T(512)(128)(4,1)S(1)}, pred[40]{0:T(512)(128)(4,1)}, u32[]{:S(2)}) copy-start(pred[40]{0:T(512)(128)(4,1)} %get-tuple-element.266) | copy-start | bytes 124
  231.3 128.0 %copy-start.17 = (pred[40,4608]{1,0:T(8,128)(4,1)S(1)}, pred[40,4608]{1,0:T(8,128)(4,1)}, u32[]{:S(2)}) copy-start(pred[40,4608]{1,0:T(8,128)(4,1)} %iota_compare_fusion.1) | copy-start | bytes 552964
  231.3 128.0 %copy-start.23 = (s32[4,4608]{1,0:T(4,128)S(1)}, s32[4,4608]{1,0:T(4,128)}, u32[]{:S(2)}) copy-start(s32[4,4608]{1,0:T(4,128)} %iota_multiply_fusion.1) | copy-start | bytes 221188
  231.3 128.0 %copy-start.70 = (f32[40]{0:T(128)S(1)}, f32[40]{0:T(128)}, u32[]{:S(2)}) copy-start(f32[40]{0:T(128)} %get-tuple-element.256) | copy-start | bytes 484
  231.3 128.0 %copy-start.71 = (s32[40]{0:T(128)S(1)}, s32[40]{0:T(128)}, u32[]{:S(2)}) copy-start(s32[40]{0:T(128)} %get-tuple-element.257) | copy-start | bytes 484
  231.3 128.0 %copy-start.72 = (pred[40]{0:T(512)(128)(4,1)S(1)}, pred[40]{0:T(512)(128)(4,1)}, u32[]{:S(2)}) copy-start(pred[40]{0:T(512)(128)(4,1)} %get-tuple-element.265) | copy-start | bytes 124
  290.3 149.0 %copy-start.16 = (pred[40,5248]{1,0:T(8,128)(4,1)S(1)}, pred[40,5248]{1,0:T(8,128)(4,1)}, u32[]{:S(2)}) copy-start(pred[40,5248]{1,0:T(8,128)(4,1)} %iota_compare_fusion) | copy-start | bytes 629764
  290.3 149.0 %copy-start.21 = (s32[4,5248]{1,0:T(4,128)S(1)}, s32[4,5248]{1,0:T(4,128)}, u32[]{:S(2)}) copy-start(s32[4,5248]{1,0:T(4,128)} %iota_multiply_fusion) | copy-start | bytes 251908
  290.3 149.0 %copy-start.76 = (s32[40]{0:T(128)S(1)}, s32[40]{0:T(128)}, u32[]{:S(2)}) copy-start(s32[40]{0:T(128)} %get-tuple-element.230) | copy-start | bytes 484
  290.4 149.0 %copy-start.77 = (f32[40]{0:T(128)S(1)}, f32[40]{0:T(128)}, u32[]{:S(2)}) copy-start(f32[40]{0:T(128)} %get-tuple-element.231) | copy-start | bytes 484
  290.4 149.0 %copy-start.78 = (pred[40]{0:T(512)(128)(4,1)S(1)}, pred[40]{0:T(512)(128)(4,1)}, u32[]{:S(2)}) copy-start(pred[40]{0:T(512)(128)(4,1)} %get-tuple-element.264) | copy-start | bytes 124
  359.3 171.1 %copy-start.60 = (f32[4,40]{1,0:T(4,128)S(1)}, f32[4,40]{1,0:T(4,128)}, u32[]{:S(2)}) copy-start(f32[4,40]{1,0:T(4,128)} %copy.150) | copy-start | bytes 1924
  359.3 171.1 %copy-start.61 = (f32[4,40]{1,0:T(4,128)S(1)}, f32[4,40]{1,0:T(4,128)}, u32[]{:S(2)}) copy-start(f32[4,40]{1,0:T(4,128)} %copy.114) | copy-start | bytes 1924
  359.3 171.1 %copy-start.62 = (f32[4,40]{1,0:T(4,128)S(1)}, f32[4,40]{1,0:T(4,128)}, u32[]{:S(2)}) copy-start(f32[4,40]{1,0:T(4,128)} %copy.120) | copy-start | bytes 1924
  359.3 171.1 %copy-start.63 = (f32[4,40]{1,0:T(4,128)S(1)}, f32[4,40]{1,0:T(4,128)}, u32[]{:S(2)}) copy-start(f32[4,40]{1,0:T(4,128)} %copy.126) | copy-start | bytes 1924
  359.3 171.1 %copy-start.64 = (f32[4,40]{1,0:T(4,128)S(1)}, f32[4,40]{1,0:T(4,128)}, u32[]{:S(2)}) copy-start(f32[4,40]{1,0:T(4,128)} %copy.132) | copy-start | bytes 1924
  359.3 171.1 %copy-start.65 = (f32[4,40]{1,0:T(4,128)S(1)}, f32[4,40]{1,0:T(4,128)}, u32[]{:S(2)}) copy-start(f32[4,40]{1,0:T(4,128)} %copy.138) | copy-start | bytes 1924
  359.4 171.1 %copy-start.66 = (f32[4,40]{1,0:T(4,128)S(1)}, f32[4,40]{1,0:T(4,128)}, u32[]{:S(2)}) copy-start(f32[4,40]{1,0:T(4,128)} %copy.144) | copy-start | bytes 1924
  359.4 171.1 %copy-start.67 = (f32[4,40]{1,0:T(4,128)S(1)}, f32[4,40]{1,0:T(4,128)}, u32[]{:S(2)}) copy-start(f32[4,40]{1,0:T(4,128)} %copy.108) | copy-start | bytes 1924
  359.4 171.1 %copy-start.69 = (f32[2]{0:T(128)S(1)}, f32[2]{0:T(128)}, u32[]{:S(2)}) copy-start(f32[2]{0:T(128)} %constant.153.clone) | copy-start | bytes 28
  540.7 12.8 %copy-start.34 = (bf16[4,2,4,3,2,40]{5,2,4,3,1,0:T(4,128)(2,1)S(1)}, bf16[4,2,4,3,2,40]{5,2,4,3,1,0:T(4,128)(2,1)}, u32[]{:S(2)}) copy-start(bf16[4,2,4,3,2,40]{5,2,4,3,1,0:T(4,128)(2,1)} %get-tuple-element.180) | copy-start | bytes 46084
  563.3 22.0 %copy-start.33 = (bf16[4,2,4,3,2,40]{5,2,4,3,1,0:T(4,128)(2,1)S(1)}, bf16[4,2,4,3,2,40]{5,2,4,3,1,0:T(4,128)(2,1)}, u32[]{:S(2)}) copy-start(bf16[4,2,4,3,2,40]{5,2,4,3,1,0:T(4,128)(2,1)} %get-tuple-element.179) | copy-start | bytes 46084
  598.3 28.3 %copy-start.32 = (bf16[4,2,4,3,2,40]{5,2,4,3,1,0:T(4,128)(2,1)S(1)}, bf16[4,2,4,3,2,40]{5,2,4,3,1,0:T(4,128)(2,1)}, u32[]{:S(2)}) copy-start(bf16[4,2,4,3,2,40]{5,2,4,3,1,0:T(4,128)(2,1)} %get-tuple-element.178) | copy-start | bytes 46084
  642.1 39.5 %copy-start.31 = (bf16[4,2,4,3,2,40]{5,2,4,3,1,0:T(4,128)(2,1)S(1)}, bf16[4,2,4,3,2,40]{5,2,4,3,1,0:T(4,128)(2,1)}, u32[]{:S(2)}) copy-start(bf16[4,2,4,3,2,40]{5,2,4,3,1,0:T(4,128)(2,1)} %get-tuple-element.177) | copy-start | bytes 46084
  700.5 6.9 copy-start.7
  700.5 6.9 copy-start.8
  700.5 6.9 copy-start.45
  753.3 12.6 %copy-start.38 = (f32[40,2]{1,0:T(8,128)S(1)}, f32[40,2]{1,0:T(8,128)}, u32[]{:S(2)}) copy-start(f32[40,2]{1,0:T(8,128)} %copy.140) | copy-start | bytes 964
  774.1 8.5 copy-start.5
  774.1 8.5 copy-start.6
  774.1 8.5 copy-start.44
  838.0 11.3 %copy-start.37 = (f32[40,2]{1,0:T(8,128)S(1)}, f32[40,2]{1,0:T(8,128)}, u32[]{:S(2)}) copy-start(f32[40,2]{1,0:T(8,128)} %copy.146) | copy-start | bytes 964
  859.0 10.1 copy-start.3
  859.1 10.1 copy-start.4
  859.1 10.1 copy-start.43
  869.1 63.5 %copy-start.30 = (bf16[4,2,4,3,2,40]{5,2,4,3,1,0:T(4,128)(2,1)S(1)}, bf16[4,2,4,3,2,40]{5,2,4,3,1,0:T(4,128)(2,1)}, u32[]{:S(2)}) copy-start(bf16[4,2,4,3,2,40]{5,2,4,3,1,0:T(4,128)(2,1)} %get-tuple-element.174) | copy-start | bytes 46084
  933.9 12.9 %copy-start.36 = (f32[40,2]{1,0:T(8,128)S(1)}, f32[40,2]{1,0:T(8,128)}, u32[]{:S(2)}) copy-start(f32[40,2]{1,0:T(8,128)} %copy.152) | copy-start | bytes 964
  956.6 13.3 %copy-start.1 = (bf16[40,1,4,5248]{3,2,1,0:T(4,128)(2,1)S(1)}, bf16[40,1,4,5248]{3,2,1,0:T(4,128)(2,1)}, u32[]{:S(2)}) copy-start(bf16[40,1,4,5248]{3,2,1,0:T(4,128)(2,1)} %get-tuple-element.162) | copy-start | bytes 5038084
  956.6 13.3 %copy-start.2 = (bf16[40,1,4,5248]{3,2,1,0:T(4,128)(2,1)S(1)}, bf16[40,1,4,5248]{3,2,1,0:T(4,128)(2,1)}, u32[]{:S(2)}) copy-start(bf16[40,1,4,5248]{3,2,1,0:T(4,128)(2,1)} %get-tuple-element.163) | copy-start | bytes 5038084
  956.6 13.3 %copy-start.42 = (f32[4,2,2,40]{0,1,2,3:T(2,128)S(1)}, f32[4,2,2,40]{0,1,2,3:T(2,128)}, u32[]{:S(2)}) copy-start(f32[4,2,2,40]{0,1,2,3:T(2,128)} %broadcast_multiply_fusion) | copy-start | bytes 7684
  969.9 72.9 %copy-start.24 = (bf16[4,2,4,4,2,40]{5,3,4,2,1,0:T(4,128)(2,1)S(1)}, bf16[4,2,4,4,2,40]{5,3,4,2,1,0:T(4,128)(2,1)}, u32[]{:S(2)}) copy-start(bf16[4,2,4,4,2,40]{5,3,4,2,1,0:T(4,128)(2,1)} %copy.113) | copy-start | bytes 61444
  969.9 72.9 %copy-start.25 = (bf16[4,2,4,4,2,40]{5,3,4,2,1,0:T(4,128)(2,1)S(1)}, bf16[4,2,4,4,2,40]{5,3,4,2,1,0:T(4,128)(2,1)}, u32[]{:S(2)}) copy-start(bf16[4,2,4,4,2,40]{5,3,4,2,1,0:T(4,128)(2,1)} %copy.119) | copy-start | bytes 61444
  969.9 72.9 %copy-start.26 = (bf16[4,2,4,4,2,40]{5,3,4,2,1,0:T(4,128)(2,1)S(1)}, bf16[4,2,4,4,2,40]{5,3,4,2,1,0:T(4,128)(2,1)}, u32[]{:S(2)}) copy-start(bf16[4,2,4,4,2,40]{5,3,4,2,1,0:T(4,128)(2,1)} %copy.125) | copy-start | bytes 61444
  969.9 72.9 %copy-start.27 = (bf16[4,2,4,4,2,40]{5,3,4,2,1,0:T(4,128)(2,1)S(1)}, bf16[4,2,4,4,2,40]{5,3,4,2,1,0:T(4,128)(2,1)}, u32[]{:S(2)}) copy-start(bf16[4,2,4,4,2,40]{5,3,4,2,1,0:T(4,128)(2,1)} %copy.131) | copy-start | bytes 61444
  969.9 80.2 %copy-start.20 = (f32[1,2,1280]{2,1,0:T(2,128)S(1)}, f32[1,2,1280]{2,1,0:T(2,128)}, u32[]{:S(2)}) copy-start(f32[1,2,1280]{2,1,0:T(2,128)} %custom-call) | copy-start | bytes 30724
  1045.0 15.7 %all-to-all-start.1 = ((bf16[4,2,4,4,2,320,1]{5,3,6,4,2,1,0:T(4,128)(2,1)}), bf16[4,2,4,4,2,320,1]{5,3,6,4,2,1,0:T(4,128)(2,1)S(1)}, u32[]{:S(2)}, u32[]{:S(2)}) async-start(bf16[4,2,4,4,2,320,1]{5,3,6,4,2,1,0:T(4,128)(2,1)} %bitcast.79), calls=%async_computation.1 | async-start | bytes 393216 | tf_op jit(solution)/shard_map/all_to_all | solution.py:153
  (18 other events, 56.9 us)
where the time goes:
time: 1090 us; the launch traced here: 1080 us
  other arithmetic  568 us (52%)
  matrix products  382 us (35%)
  local copies, waits for them, and re-layouts  109 us (10%)
  starting transfers between devices  11.4 us (1%)
    another operation x16, other arithmetic  472 us
    dot_general x8, matrix products, on_device(): jnp.einsum('jelqx,jrkx->kelqrj', tendency, tables, preferred_element_type...  317 us
    dot_general x8, matrix products, on_device(): jnp.einsum('kelfrj,jrkx->jelfx', coeff_block, tables, preferred_element_t...  63.2 us
    another operation x8, other arithmetic, tendency_terms(): jnp.stack([-absolute * spreading_rate_grid, absolute * vorticity, 0.5 * (...  52.4 us
  transfers between devices with their start and end apart: 2, of which 0 were waited for; matrix products, arithmetic and copies ran while one was open for 47% of the time, Pallas kernels for 0%

commit v1 on v0

v1 whole, which is shorter than its diff:
```python
import jax
import jax.numpy as jnp
from jax import lax
from jax.sharding import PartitionSpec as P

TWO_PI = 6.283185307179586


def on_device(spectra, legendre, assignment, circle_longitudes, coriolis, weights, thickness):
    levels = spectra.shape[1]
    coeff_count = spectra.shape[4]
    lat_half = legendre.shape[2]
    band_count = lax.axis_size("band")
    band_place = lax.axis_index("band")
    wave_total = spectra.shape[0] * band_count
    stride = coeff_count // wave_total
    slots = lat_half // band_count
    pairs = 2 * levels
    own_wave = stride * lax.dynamic_slice_in_dim(assignment, band_place, 1)[0]
    index = jnp.arange(coeff_count, dtype=jnp.int32)
    parity = jnp.where(index % 2 == 0, 1.0, -1.0).astype(jnp.float32)
    inside = index < coeff_count - own_wave
    real_ok = (jnp.arange(2) == 0) | (own_wave > 0)
    keeper = inside[None, :] & real_ok[:, None]
    masked = jnp.where(keeper, spectra[0], jnp.zeros_like(spectra[0]))
    ordered = jnp.transpose(masked, (1, 2, 0, 3))
    stacked = jnp.stack([ordered, ordered * parity.astype(jnp.bfloat16)], axis=2)
    stacked = stacked.reshape(6 * pairs, coeff_count)
    fourier = jnp.dot(stacked, legendre[0], preferred_element_type=jnp.float32)
    fourier = fourier.astype(jnp.bfloat16)
    outgoing = jnp.transpose(fourier.reshape(6 * pairs, band_count, slots), (1, 0, 2))
    arrived = lax.all_to_all(outgoing, "band", split_axis=0, concat_axis=0, tiled=True)

    first = band_place * slots
    counts = lax.dynamic_slice_in_dim(circle_longitudes, first, slots)
    planet = lax.dynamic_slice_in_dim(coriolis, first, slots, axis=1)
    quad = lax.dynamic_slice_in_dim(weights, first, slots, axis=1)
    most = 3 * (wave_total - 1) + 1
    ratio = counts // stride
    aliased = (ratio * stride == counts) & (ratio < most)
    points = jnp.where(aliased, ratio, most)
    xs = jnp.arange(most, dtype=jnp.int32)
    phase = (assignment[:, None, None] * xs[None, :, None]) % points[None, None, :]
    angles = TWO_PI * phase.astype(jnp.float32) / points.astype(jnp.float32)
    live = xs[None, :, None] < points[None, None, :]
    tables = jnp.stack(
        [jnp.where(live, jnp.cos(angles), 0.0), jnp.where(live, -jnp.sin(angles), 0.0)], axis=1
    )
    waves = stride * assignment
    resolved = 2 * waves[:, None] < counts[None, :]
    gain = jnp.where(resolved, jnp.where(waves[:, None] == 0, 1.0, 2.0), 0.0)
    coeffs = arrived.astype(jnp.float32).reshape(wave_total, 3, 2, pairs, slots)
    coeffs = coeffs * gain[:, None, None, None, :]
    grid = jnp.sum(
        coeffs[:, :, :, None] * tables[:, None, :, :, None, :], axis=(0, 2)
    )
    vort, div, theta = grid[0], grid[1], grid[2]
    spin = jnp.broadcast_to(planet[:, None, :], (2, levels, slots)).reshape(pairs, slots)
    absolute = vort + spin
    terms = jnp.stack(
        [-absolute * div, absolute * vort, 0.5 * (vort * vort + div * div), -theta * div]
    )
    summed = jnp.sum(
        terms[None, :, None] * tables[:, None, :, :, None, :], axis=3
    )
    quad = jnp.broadcast_to(quad[:, None, :], (2, levels, slots)).reshape(pairs, slots)
    scale = jnp.where(resolved, 1.0 / points.astype(jnp.float32), 0.0)[:, None, :] * quad
    returned = (summed * scale[:, None, None]).astype(jnp.bfloat16)
    returned = returned.reshape(wave_total, 8 * pairs, slots)
    landed = lax.all_to_all(returned, "band", split_axis=0, concat_axis=0, tiled=True)
    landed = jnp.transpose(landed, (1, 0, 2)).reshape(8 * pairs, lat_half)
    projected = lax.dot_general(
        landed, legendre[0], (((1,), (1,)), ((), ())), preferred_element_type=jnp.float32
    ).reshape(4, 2, 2, levels, coeff_count)
    combined = projected[:, :, 0] + parity * projected[:, :, 1]

    weighted = ordered[2].astype(jnp.float32) * thickness[None, :, None]
    partial = [weighted[:, levels - 1]]
    for level in range(levels - 2, -1, -1):
        partial.insert(0, partial[0] + weighted[:, level])
    group = lax.axis_size(("fld", "sub"))
    sums = lax.all_gather(partial[0], ("fld", "sub"))
    later = jnp.arange(group) > lax.axis_index(("fld", "sub"))
    below = jnp.sum(jnp.where(later[:, None, None], sums, 0.0), axis=0)
    column = jnp.stack(partial, axis=1) + below[:, None]
    degree = own_wave + index
    truncation = coeff_count - 1
    laplace = (degree * (degree + 1)).astype(jnp.float32) / float(truncation * (truncation + 1))
    divergence = combined[1] + laplace * (column + combined[2])
    result = jnp.stack([combined[0], divergence, combined[3]])
    result = jnp.where(keeper[None, :, None, :], result, 0.0).astype(jnp.bfloat16)
    return jnp.transpose(result, (2, 0, 1, 3))[None]


def solution(mesh):
    in_specs = (
        P(("member", "band"), ("fld", "sub"), None, None, None),
        P("band", None, None),
        P(),
        P(),
        P(),
        P(),
        P(("fld", "sub")),
    )
    out_specs = P(("member", "band"), ("fld", "sub"), None, None, None)
    return jax.shard_map(
        on_device, mesh=mesh, in_specs=in_specs, out_specs=out_specs, check_vma=False
    )
```

time: 1090 us -> 40.9 us (0.04); the launches traced: 1080 us -> 40.3 us
  other arithmetic: 568 us -> 11.5 us
  matrix products: 382 us -> 2.53 us
  local copies, waits for them, and re-layouts: 109 us -> 7.92 us
    another operation x27 -> x6, other arithmetic: 526 us -> 3.16 us  [the longest x3 2.48 us: on_device(): jnp.stack([ordered, ordered * parity.astype(jnp.bfloat16)], axis=2)]
    dot_general x18 -> x2, matrix products: 382 us -> 2.53 us  [the longest x1 1.35 us: on_device(): fourier = jnp.dot(stacked, legendre[0], preferred_element_type=jnp.float32)]
    mul x25 -> x1, local copies, waits for them, and re-layouts: 42.5 us -> 0.01 us  [on_device(): jnp.where(resolved, 1.0 / points.astype(jnp.float32), 0.0)[:, None, :]]
    mul x19 -> x6, other arithmetic: 21.6 us -> 2.57 us  [the longest x1 0.93 us: on_device(): coeffs = coeffs * gain[:, None, None, None, :]]
    reshape x5 -> x3, local copies, waits for them, and re-layouts: 18.2 us -> 1.78 us  [the longest x2 1.75 us: on_device(): fourier.reshape(6 * pairs, band_count, slots)]
    another operation x2 -> x1, local copies, waits for them, and re-layouts: 14.8 us -> 0.04 us  [on_device(): jnp.stack([ordered, ordered * parity.astype(jnp.bfloat16)], axis=2)]
  transfers between devices with their start and end apart: 2 -> 2, of which waited for: 0 -> 1; matrix products, arithmetic and copies ran while one was open for 47% -> 18% of each run, Pallas kernels for 0% -> 0%
where the time goes in v1:
time: 40.9 us; the launch traced here: 40.3 us
  other arithmetic  11.5 us (28%)
  starting transfers between devices  11.4 us (28%)
  local copies, waits for them, and re-layouts  7.92 us (19%)
  blocking collectives  5.2 us (13%)
  matrix products  2.53 us (6%)
  between operations  0.97 us (2%)
  waiting for transfers between devices  0.71 us (2%)
    all_to_all x1, starting transfers between devices, on_device(): lax.all_to_all(outgoing, 'band', split_axis=0, concat_axis=0, tiled=True)  6.33 us
    all_gather x1, blocking collectives, on_device(): sums = lax.all_gather(partial[0], ('fld', 'sub'))  5.2 us
    all_to_all x1, starting transfers between devices, on_device(): lax.all_to_all(returned, 'band', split_axis=0, concat_axis=0, tiled=True)  5.09 us
    another operation x3, other arithmetic, on_device(): jnp.stack([ordered, ordered * parity.astype(jnp.bfloat16)], axis=2)  2.48 us
    reshape x2, local copies, waits for them, and re-layouts, on_device(): fourier.reshape(6 * pairs, band_count, slots)  1.75 us
    select_n x1, other arithmetic, on_device(): jnp.where(live, jnp.cos(angles), 0.0)  1.41 us
    dynamic_slice x1, local copies, waits for them, and re-layouts, on_device(): own_wave = stride * lax.dynamic_slice_in_dim(assignment, band_place, 1)[0]  1.39 us
    dot_general x1, matrix products, on_device(): fourier = jnp.dot(stacked, legendre[0], preferred_element_type=jnp.float32)  1.35 us
  transfers between devices with their start and end apart: 2, of which 1 were waited for; matrix products, arithmetic and copies ran while one was open for 18% of the time, Pallas kernels for 0%

profile of v1, /device:TPU:0, one launch (start us, length us, event | category | flops | bytes accessed | tf_op | source)
XLA Modules:
  0.0 40.3 jit_solution(11909256079594735282)
XLA Ops:
  0.0 0.0 copy-start
  0.0 0.0 copy-start.11
  0.0 0.0 copy-start.10
  0.0 1.4 %dynamic_slice.12 = s32[1]{0:T(128)} dynamic-slice(s32[4]{0:T(128)} %param.9, s32[]{:T(128)S(6)} %select_n.121), dynamic_slice_sizes={1} | dynamic-slice | bytes 12 | tf_op jit(solution)/shard_map/dynamic_slice | solution.py:19
  2.1 0.1 broadcast_and_fusion
  2.2 0.0 copy-start.5
  2.2 0.9 %fusion.20 = bf16[3,2,1,4,1280]{4,3,1,0,2:T(4,128)(2,1)S(1)} fusion(bf16[1,4,3,2,1280]{4,3,2,1,0:T(2,128)(2,1)} %param.7, pred[2,1280]{1,0:T(4,128)(4,1)S(1)} %broadcast_and_fusion), kind=kLoop, calls=%fused_computation.45 | loop fusion | flops 30720 | bytes 125440 | tf_op jit(solution)/shard_map/stack | solution.py:27
  3.1 1.5 %multiply_bitcast_fusion = (bf16[3,2,1,4,1280]{4,3,1,0,2:T(4,128)(2,1)S(1)}, bf16[3,2,4,1280]{3,2,1,0:T(4,128)(2,1)}) fusion(bf16[1280]{0:T(1024)(128)(2,1)S(1)} %fusion.29, bf16[1,4,3,2,1280]{4,3,2,1,0:T(2,128)(2,1)} %param.7, pred[2,1280]{1,0:T(4,128)(4,1)S(1)} %broadcast_and_fusion), kind=kLoop, calls=%fused_computation.37 | loop fusion | flops 61440 | bytes 189440 | tf_op jit(solution)/shard_map/stack | solution.py:27
  4.6 0.0 copy-done.5
  4.6 0.1 pad_maximum_fusion.2
  4.8 0.0 copy-done
  4.8 1.3 %fusion.4 = bf16[48,1280]{1,0:T(8,128)(2,1)} fusion(bf16[48,1280]{1,0:T(8,128)(2,1)S(1)} %reshape.360, bf16[1,1280,1280]{2,1,0:T(8,128)(2,1)S(1)} %copy-done), kind=kOutput, calls=%fused_computation.6 | convolution fusion | flops 157347840 | bytes 3522560 | tf_op jit(solution)/shard_map/dot_general | solution.py:29
  6.1 1.1 %reshape.361 = bf16[48,4,320]{2,1,0:T(4,128)(2,1)S(1)} reshape(bf16[48,1280]{1,0:T(8,128)(2,1)} %fusion.4) | data formatting | bytes 245760 | tf_op jit(solution)/shard_map/reshape | solution.py:31
  7.2 0.7 %copy.39 = bf16[48,4,320]{2,0,1:T(8,128)(2,1)} copy(bf16[48,4,320]{2,1,0:T(4,128)(2,1)S(1)} %reshape.361) | data formatting | bytes 245760 | tf_op jit(solution)/shard_map/reshape | solution.py:31
  7.9 6.3 %all-to-all-start = ((bf16[4,48,320]{2,1,0:T(8,128)(2,1)}), bf16[4,48,320]{2,1,0:T(8,128)(2,1)}, u32[]{:S(2)}, u32[]{:S(2)}) async-start(bf16[4,48,320]{2,1,0:T(8,128)(2,1)} %bitcast.62), calls=%async_computation | async-start | bytes 294912 | tf_op jit(solution)/shard_map/all_to_all | solution.py:32
  14.2 0.8 %broadcast_divide_fusion = (f32[320]{0:T(512)S(1)}, s32[320]{0:T(512)S(1)}, s32[320]{0:T(512)S(1)}) fusion(s32[1280]{0:T(1024)} %param.10, s32[]{:T(128)S(6)} %select_n.125), kind=kLoop, calls=%fused_computation.80 | loop fusion | flops 4800 | bytes 5124 | tf_op jit(solution)/shard_map/div | solution.py:67
  15.0 0.0 copy-done.11
  15.0 0.1 iota_multiply_fusion
  15.1 0.6 %fusion.28 = f32[1280]{0:T(1024)} fusion(), kind=kLoop, calls=%fused_computation.64 | loop fusion | flops 10240 | bytes 5120 | tf_op jit(solution)/shard_map/jit(_where)/select_n | solution.py:21
  15.7 0.8 %constant_dynamic-slice_fusion = (f32[2,320]{1,0:T(2,128)S(1)}, f32[2,320]{1,0:T(2,128)S(1)}) fusion(f32[2,1280]{1,0:T(2,128)} %param.12, s32[]{:T(128)S(6)} %select_n.125, f32[2,1280]{1,0:T(2,128)} %param.11), kind=kLoop, calls=%fused_computation.83 | loop fusion | bytes 10244 | tf_op jit(solution)/shard_map/dynamic_slice | solution.py:37
  16.5 0.6 %add.153 = f32[8,320]{1,0:T(8,128)} reshape(f32[2,4,320]{2,1,0:T(4,128)S(1)} %broadcast_in_dim.136) | data formatting | bytes 20480 | tf_op jit(solution)/shard_map/add | solution.py:59
  17.1 0.0 copy-done.10
  17.1 0.8 %convert_multiply_fusion.1 = f32[2,4,1280]{2,1,0:T(4,128)S(1)} fusion(bf16[3,2,4,1280]{3,2,1,0:T(4,128)(2,1)} %get-tuple-element.11, f32[4]{0:T(128)S(1)} %copy-done.10), kind=kLoop, calls=%fused_computation.43 | loop fusion | flops 20480 | bytes 61456 | tf_op jit(solution)/shard_map/mul | solution.py:77
  18.0 0.0 copy-start.3
  18.0 0.0 copy-start.1
  18.0 0.6 %copy-done.3 = f32[2,1,1280]{2,1,0:T(1,128)} copy-done((f32[2,1,1280]{2,1,0:T(1,128)}, f32[2,1,1280]{2,1,0:T(1,128)S(1)}, u32[]{:S(2)}) %copy-start.3) | copy-done | bytes 10264
  18.6 0.6 %fusion.33 = (f32[1,2,1,1280]{3,2,1,0:T(1,128)}, f32[1,2,1,1280]{3,2,1,0:T(1,128)}) fusion(f32[2,1,1280]{2,1,0:T(1,128)S(1)} %get-tuple-element.6, f32[2,4,1280]{2,1,0:T(4,128)S(1)} %convert_multiply_fusion.1), kind=kLoop, calls=%fused_computation.86 | loop fusion | flops 2560 | bytes 51200 | tf_op jit(solution)/shard_map/stack | solution.py:85
  19.2 1.4 %cosine_select_fusion = (f32[4,1,10,320]{3,2,1,0:T(8,128)S(1)}, f32[4,1,10,320]{3,2,1,0:T(8,128)S(1)}) fusion(f32[320]{0:T(512)S(1)} %get-tuple-element.26, pred[320]{0:T(512)(128)(4,1)S(1)} %broadcast_compare_fusion, s32[320]{0:T(512)S(1)} %get-tuple-element.25, s32[4,10]{1,0:T(4,128)S(1)} %iota_multiply_fusion, pred[10,320]{1,0:T(8,128)(4,1)S(1)} %iota_compare_fusion), kind=kLoop, calls=%fused_computation.33 | loop fusion | flops 166400 | bytes 108640 | tf_op jit(solution)/shard_map/jit(_where)/select_n | solution.py:47
  20.6 0.1 compare_select_fusion
  20.7 0.0 all-to-all-done
  20.7 0.9 %convert_multiply_fusion = f32[4,3,2,8,320]{4,3,2,1,0:T(8,128)S(1)} fusion(bf16[4,3,2,8,320]{4,3,2,1,0:T(8,128)(2,1)} %bitcast.22, f32[4,320]{1,0:T(4,128)S(1)} %get-tuple-element.24), kind=kLoop, calls=%fused_computation.9 | loop fusion | flops 122880 | bytes 373760 | tf_op jit(solution)/shard_map/mul | solution.py:53
  21.7 0.2 multiply_reduce_fusion.1
  21.9 0.8 %fusion.9 = (f32[1,10,8,320]{3,2,1,0:T(8,128)S(1)}, f32[1,10,8,320]{3,2,1,0:T(8,128)S(1)}, f32[1,10,8,320]{3,2,1,0:T(8,128)S(1)}, f32[1,10,8,320]{3,2,1,0:T(8,128)S(1)}) fusion(f32[3,10,8,320]{3,2,1,0:T(8,128)S(1)} %multiply_reduce_fusion.1, f32[8,320]{1,0:T(8,128)} %add.153), kind=kLoop, calls=%fused_computation.22 | loop fusion | flops 256000 | bytes 727040 | tf_op jit(solution)/shard_map/mul | solution.py:61
  22.7 0.3 multiply_reduce_fusion
  23.0 0.7 %multiply_convert_fusion = bf16[4,4,2,8,320]{4,3,2,1,0:T(8,128)(2,1)} fusion(f32[4,4,2,8,320]{4,3,2,1,0:T(8,128)S(1)} %multiply_reduce_fusion, f32[4,8,320]{2,1,0:T(8,128)S(1)} %broadcast_multiply_fusion), kind=kLoop, calls=%fused_computation.8 | loop fusion | flops 163840 | bytes 532480 | tf_op jit(solution)/shard_map/convert_element_type | solution.py:68
  23.7 5.1 %all-to-all-start.1 = ((bf16[4,64,320]{2,1,0:T(8,128)(2,1)}), bf16[4,64,320]{2,1,0:T(8,128)(2,1)S(1)}, u32[]{:S(2)}, u32[]{:S(2)}) async-start(bf16[4,64,320]{2,1,0:T(8,128)(2,1)} %bitcast.64), calls=%async_computation.1 | async-start | bytes 393216 | tf_op jit(solution)/shard_map/all_to_all | solution.py:70
  28.8 0.5 %iota_compare_fusion.2 = pred[4]{0:T(512)(128)(4,1)} fusion(s32[]{:T(128)S(6)} %add.164), kind=kLoop, calls=%fused_computation.82 | loop fusion | flops 4 | bytes 8 | tf_op jit(solution)/shard_map/gt | solution.py:83
  29.4 0.0 copy-done.1
  29.4 5.2 %all-gather = f32[8,1,1280]{2,1,0:T(1,128)S(1)} all-gather(f32[2,1,1280]{2,1,0:T(1,128)S(1)} %get-tuple-element.5), channel_id=2, replica_groups=mesh['member'=2,'band'=4,'fld'=2,'sub'=2] {'fld','sub'}, dimensions={0}, use_global_device_ids=true | all-gather | bytes 51200 | tf_op jit(solution)/shard_map/all_gather | solution.py:82
  34.6 0.1 reduce
  34.7 0.7 %select_reduce_fusion = f32[2,1280]{1,0:T(2,128)S(1)} fusion(f32[4,2,1280]{2,1,0:T(2,128)S(1)} %reshape.367, pred[4]{0:T(512)(128)(4,1)} %iota_compare_fusion.2), kind=kLoop, calls=%fused_computation.44 | loop fusion | flops 17920 | bytes 51204 | tf_op jit(solution)/shard_map/reduce_sum | solution.py:84
  35.4 0.7 %all-to-all-done.1 = bf16[4,64,320]{2,1,0:T(8,128)(2,1)S(1)} async-done(((bf16[4,64,320]{2,1,0:T(8,128)(2,1)}), bf16[4,64,320]{2,1,0:T(8,128)(2,1)S(1)}, u32[]{:S(2)}, u32[]{:S(2)}) %all-to-all-start.1) | async-done | bytes 163872 | tf_op jit(solution)/shard_map/all_to_all | solution.py:70
  36.1 0.8 %copy.26 = bf16[64,4,320]{2,1,0:T(4,128)(2,1)} copy(bf16[64,4,320]{2,0,1:T(8,128)(2,1)S(1)} %bitcast.63) | data formatting | bytes 327680 | tf_op jit(solution)/shard_map/transpose | solution.py:71
  37.0 1.1 %dot_general.9 = bf16[4,2,2,4,1280]{4,3,2,1,0:T(4,128)(2,1)S(1)} reshape(bf16[64,4,320]{2,1,0:T(4,128)(2,1)} %copy.26) | data formatting | bytes 327680 | tf_op jit(solution)/shard_map/dot_general | solution.py:72
  38.1 0.0 copy-start.9
  38.1 0.0 copy-start.2
  38.1 0.0 copy-start.4
  38.1 0.0 copy-start.7
  38.1 0.0 copy-start.8
  38.1 0.0 copy-start.6
  38.2 1.2 %fusion = f32[4,2,2,4,1280]{4,3,2,1,0:T(4,128)S(1)} fusion(bf16[4,2,2,4,1280]{4,3,2,1,0:T(4,128)(2,1)S(1)} %dot_general.9, bf16[1,1280,1280]{2,1,0:T(8,128)(2,1)S(1)} %copy-done), kind=kOutput, calls=%fused_computation.1 | convolution fusion | flops 209715200 | bytes 3768320 | tf_op jit(solution)/shard_map/dot_general | solution.py:72
  39.3 0.0 copy-done.9
  39.4 0.0 copy-done.2
  39.4 0.0 copy-done.4
  39.4 0.0 copy-done.7
  39.4 0.0 copy-done.8
  39.5 0.1 fusion.36
  39.5 0.0 copy-done.6
  39.6 0.7 %copy.28 = bf16[1,4,3,2,1280]{4,3,2,1,0:T(2,128)(2,1)} copy(bf16[1,4,3,2,1280]{4,1,3,2,0:T(4,128)(2,1)S(1)} %fusion.17) | data formatting | bytes 122880 | tf_op jit(solution)/shard_map/broadcast_in_dim | solution.py:92
  (21 shorter events, 0.4 us)
Async XLA Ops:
  0.0 4.8 %copy-start = (bf16[1,1280,1280]{2,1,0:T(8,128)(2,1)S(1)}, bf16[1,1280,1280]{2,1,0:T(8,128)(2,1)}, u32[]{:S(2)}) copy-start(bf16[1,1280,1280]{2,1,0:T(8,128)(2,1)} %param.8) | copy-start | bytes 9830404
  0.0 15.0 %copy-start.11 = (s32[4]{0:T(128)S(1)}, s32[4]{0:T(128)}, u32[]{:S(2)}) copy-start(s32[4]{0:T(128)} %param.9) | copy-start | bytes 52
  0.0 17.1 %copy-start.10 = (f32[4]{0:T(128)S(1)}, f32[4]{0:T(128)}, u32[]{:S(2)}) copy-start(f32[4]{0:T(128)} %param.13) | copy-start | bytes 52
  2.2 2.4 %copy-start.5 = (pred[2,1280]{1,0:T(4,128)(4,1)}, pred[2,1280]{1,0:T(4,128)(4,1)S(1)}, u32[]{:S(2)}) copy-start(pred[2,1280]{1,0:T(4,128)(4,1)S(1)} %broadcast_and_fusion) | copy-start | bytes 7684
  7.9 12.9 %all-to-all-start = ((bf16[4,48,320]{2,1,0:T(8,128)(2,1)}), bf16[4,48,320]{2,1,0:T(8,128)(2,1)}, u32[]{:S(2)}, u32[]{:S(2)}) async-start(bf16[4,48,320]{2,1,0:T(8,128)(2,1)} %bitcast.62), calls=%async_computation | async-start | bytes 294912 | tf_op jit(solution)/shard_map/all_to_all | solution.py:32
  18.0 0.6 %copy-start.3 = (f32[2,1,1280]{2,1,0:T(1,128)}, f32[2,1,1280]{2,1,0:T(1,128)S(1)}, u32[]{:S(2)}) copy-start(f32[2,1,1280]{2,1,0:T(1,128)S(1)} %get-tuple-element.6) | copy-start | bytes 30724
  18.0 11.4 %copy-start.1 = (f32[2,1,1280]{2,1,0:T(1,128)}, f32[2,1,1280]{2,1,0:T(1,128)S(1)}, u32[]{:S(2)}) copy-start(f32[2,1,1280]{2,1,0:T(1,128)S(1)} %get-tuple-element.5) | copy-start | bytes 30724
  23.7 12.4 %all-to-all-start.1 = ((bf16[4,64,320]{2,1,0:T(8,128)(2,1)}), bf16[4,64,320]{2,1,0:T(8,128)(2,1)S(1)}, u32[]{:S(2)}, u32[]{:S(2)}) async-start(bf16[4,64,320]{2,1,0:T(8,128)(2,1)} %bitcast.64), calls=%async_computation.1 | async-start | bytes 393216 | tf_op jit(solution)/shard_map/all_to_all | solution.py:70
  38.1 1.3 %copy-start.9 = (f32[1280]{0:T(1024)S(1)}, f32[1280]{0:T(1024)}, u32[]{:S(2)}) copy-start(f32[1280]{0:T(1024)} %fusion.28) | copy-start | bytes 15364
  38.1 1.3 %copy-start.2 = (f32[2,1,1280]{2,1,0:T(1,128)S(1)}, f32[2,1,1280]{2,1,0:T(1,128)}, u32[]{:S(2)}) copy-start(f32[2,1,1280]{2,1,0:T(1,128)} %copy-done.1) | copy-start | bytes 30724
  38.1 1.3 %copy-start.4 = (f32[2,1,1280]{2,1,0:T(1,128)S(1)}, f32[2,1,1280]{2,1,0:T(1,128)}, u32[]{:S(2)}) copy-start(f32[2,1,1280]{2,1,0:T(1,128)} %copy-done.3) | copy-start | bytes 30724
  38.1 1.3 %copy-start.7 = (f32[1,2,1,1280]{3,2,1,0:T(1,128)S(1)}, f32[1,2,1,1280]{3,2,1,0:T(1,128)}, u32[]{:S(2)}) copy-start(f32[1,2,1,1280]{3,2,1,0:T(1,128)} %get-tuple-element.19) | copy-start | bytes 30724
  38.1 1.3 %copy-start.8 = (f32[1,2,1,1280]{3,2,1,0:T(1,128)S(1)}, f32[1,2,1,1280]{3,2,1,0:T(1,128)}, u32[]{:S(2)}) copy-start(f32[1,2,1,1280]{3,2,1,0:T(1,128)} %get-tuple-element.20) | copy-start | bytes 30724
  38.1 1.4 %copy-start.6 = (pred[2,1280]{1,0:T(4,128)(4,1)S(1)}, pred[2,1280]{1,0:T(4,128)(4,1)}, u32[]{:S(2)}) copy-start(pred[2,1280]{1,0:T(4,128)(4,1)} %copy-done.5) | copy-start | bytes 7684

commit v2 on v1

v2 whole, which is shorter than its diff:
```python
import functools

import jax
import jax.numpy as jnp
from jax import lax
from jax.experimental import pallas as pl
from jax.experimental.pallas import tpu as pltpu
from jax.sharding import PartitionSpec as P

MESH = pl.DeviceIdType.MESH
COS_TERMS = (1.0, -1 / 2, 1 / 24, -1 / 720, 1 / 40320, -1 / 3628800, 1 / 479001600)
SIN_TERMS = (1.0, -1 / 6, 1 / 120, -1 / 5040, 1 / 362880, -1 / 39916800, 1 / 6227020800)
PI = 3.141592653589793


def each(count, body):
    if count <= 8:
        for i in range(count):
            body(i)
    else:

        def step(i, carry):
            body(i)
            return carry

        lax.fori_loop(0, count, step, 0)


def series(terms, square):
    value = jnp.full_like(square, terms[-1])
    for term in terms[-2::-1]:
        value = value * square + term
    return value


def circle(turns):
    half = PI * turns
    square = half * half
    sine = half * series(SIN_TERMS, square)
    cosine = series(COS_TERMS, square)
    return 1.0 - 2.0 * sine * sine, 2.0 * sine * cosine


def kernel(
    sizes, spectra, legendre, assignment, thickness, rows, out,
    table, wide, fsend, frecv, costab, sintab, coeffs, sums, bsend, brecv, proj,
    local, colsend, colrecv, load_sem, fs_sem, fr_sem, bs_sem, br_sem, cs_sem, cr_sem,
):
    band, group, subs, stride, levels, coeff, lat, block, most = sizes
    pairs = 2 * levels
    me = lax.axis_index("band")
    mine = lax.axis_index("fld") * subs + lax.axis_index("sub")

    def band_peer(k):
        return {"band": lax.rem(me + k, band)}

    def group_peer(k):
        peer = lax.rem(mine + k, group)
        return {"fld": peer // subs, "sub": lax.rem(peer, subs)}

    load = pltpu.make_async_copy(legendre.at[0], table.at[:, pl.ds(0, lat)], load_sem)
    load.start()
    barrier = pltpu.get_barrier_semaphore()

    def greet_band(k):
        pl.semaphore_signal(barrier, inc=1, device_id=band_peer(k + 1), device_id_type=MESH)

    def greet_group(k):
        pl.semaphore_signal(barrier, inc=1, device_id=group_peer(k + 1), device_id_type=MESH)

    each(band - 1, greet_band)
    each(group - 1, greet_group)

    own = stride * assignment[me]
    index = lax.broadcasted_iota(jnp.int32, (2, coeff), 1)
    part = lax.broadcasted_iota(jnp.int32, (2, coeff), 0)
    keep = (index < coeff - own) & (part * jnp.where(own == 0, 1, 0) == 0)
    parity = (1 - 2 * lax.rem(index, 2)).astype(jnp.float32)
    for level in range(levels):
        for field in range(3):
            value = jnp.where(keep, spectra[0, level, field].astype(jnp.float32), 0.0)
            other = value * parity
            for r in range(2):
                row = (2 * field + r) * pairs + level
                wide[row : row + 1, :] = value[r : r + 1]
                wide[row + levels : row + levels + 1, :] = other[r : r + 1]
    both = wide[...].astype(jnp.bfloat16)
    if block * band > lat:
        table[:, lat:] = jnp.zeros((coeff, block * band - lat), jnp.bfloat16)
    pl.semaphore_wait(barrier, band + group - 2)
    load.wait()

    def forward(k):
        return pltpu.make_async_remote_copy(
            src_ref=fsend.at[k], dst_ref=frecv.at[me], send_sem=fs_sem.at[k],
            recv_sem=fr_sem.at[k], device_id=band_peer(k + 1), device_id_type=MESH,
        )

    def back(k):
        return pltpu.make_async_remote_copy(
            src_ref=bsend.at[k], dst_ref=brecv.at[me], send_sem=bs_sem.at[k],
            recv_sem=br_sem.at[k], device_id=band_peer(k + 1), device_id_type=MESH,
        )

    def across(k):
        return pltpu.make_async_remote_copy(
            src_ref=colsend, dst_ref=colrecv.at[mine], send_sem=cs_sem.at[k],
            recv_sem=cr_sem.at[k], device_id=group_peer(k + 1), device_id_type=MESH,
        )

    def lanes(b):
        return pl.ds(pl.multiple_of(b * block, 128), block)

    def transform(b):
        return jnp.dot(both, table[:, lanes(b)], preferred_element_type=jnp.float32).astype(
            jnp.bfloat16
        )

    def send_forward(k):
        fsend[k] = transform(lax.rem(me + k + 1, band))
        forward(k).start()

    each(band - 1, send_forward)
    frecv[me] = transform(me)

    for r in range(2):
        total = None
        for level in range(levels - 1, -1, -1):
            row = (4 + r) * pairs + level
            value = thickness[level] * wide[row : row + 1, :]
            total = value if total is None else total + value
            local[r, level : level + 1, :] = total
        colsend[r : r + 1, :] = total
    each(group - 1, lambda k: across(k).start())

    points = rows[0:1, lanes(me)]
    inverse = rows[1:2, lanes(me)]
    counts = rows[2:3, lanes(me)]
    pair = lax.broadcasted_iota(jnp.int32, (pairs, block), 0)
    spin = jnp.where(pair < levels, rows[3:4, lanes(me)], rows[4:5, lanes(me)])
    quad = jnp.where(pair < levels, rows[5:6, lanes(me)], rows[6:7, lanes(me)])
    height = costab.shape[1]
    xs = lax.broadcasted_iota(jnp.int32, (height, block), 0).astype(jnp.float32)

    def fill(s):
        phase = xs * assignment[s].astype(jnp.float32)
        phase = phase - points * jnp.floor(phase * inverse)
        turns = phase * inverse
        cosine, sine = circle(turns - jnp.floor(turns + 0.5))
        costab[s] = jnp.where(xs < points, cosine, 0.0)
        sintab[s] = jnp.where(xs < points, sine, 0.0)

    each(band, fill)

    def weigh(s):
        wave = (stride * assignment[s]).astype(jnp.float32)
        gain = jnp.where(2.0 * wave < counts, jnp.where(wave == 0.0, 1.0, 2.0), 0.0)
        coeffs[s] = frecv[s].astype(jnp.float32) * gain
        sums[s] = jnp.zeros(sums.shape[1:], jnp.float32)

    each(band - 1, lambda k: forward(k).wait_recv())
    each(band, weigh)

    def sample(x, carry):
        def add_wave(s, fields):
            cosine = costab[s, pl.ds(x, 1), :]
            sine = sintab[s, pl.ds(x, 1), :]
            return tuple(
                fields[f]
                + coeffs[s, 2 * f * pairs : (2 * f + 1) * pairs, :] * cosine
                - coeffs[s, (2 * f + 1) * pairs : (2 * f + 2) * pairs, :] * sine
                for f in range(3)
            )

        fields = tuple(jnp.zeros((pairs, block), jnp.float32) for _ in range(3))
        if band <= 8:
            for s in range(band):
                fields = add_wave(s, fields)
        else:
            fields = lax.fori_loop(0, band, add_wave, fields)
        vort, div, theta = fields
        absolute = vort + spin
        terms = (
            -absolute * div,
            absolute * vort,
            0.5 * (vort * vort + div * div),
            -theta * div,
        )

        def collect(s):
            cosine = costab[s, pl.ds(x, 1), :]
            sine = sintab[s, pl.ds(x, 1), :]
            for q in range(4):
                sums[s, 2 * q * pairs : (2 * q + 1) * pairs, :] += terms[q] * cosine
                sums[s, (2 * q + 1) * pairs : (2 * q + 2) * pairs, :] -= terms[q] * sine

        each(band, collect)
        return carry

    lax.fori_loop(0, most, sample, 0)

    def finish(s):
        wave = (stride * assignment[s]).astype(jnp.float32)
        scale = jnp.where(2.0 * wave < counts, quad, 0.0)
        value = sums[s].reshape(8, pairs, block) * scale[None]
        return value.reshape(8 * pairs, block).astype(jnp.bfloat16)

    def send_back(k):
        bsend[k] = finish(lax.rem(me + k + 1, band))
        back(k).start()

    each(band - 1, send_back)
    brecv[me] = finish(me)

    def project(b):
        return lax.dot_general(
            brecv[b], table[:, lanes(b)], (((1,), (1,)), ((), ())),
            preferred_element_type=jnp.float32,
        )

    proj[...] = project(me)

    def gather_back(k):
        back(k).wait_recv()
        proj[...] += project(lax.rem(me + band - k - 1, band))

    each(band - 1, gather_back)
    each(group - 1, lambda k: across(k).wait_recv())
    below = jnp.zeros((2, coeff), jnp.float32)
    for k in range(group - 1):
        sender = lax.rem(mine + group - k - 1, group)
        below = below + jnp.where(sender > mine, 1.0, 0.0) * colrecv[sender]
    degree = own + index[0:1]
    laplace = (degree * (degree + 1)).astype(jnp.float32) * (1.0 / float((coeff - 1) * coeff))
    sign = parity[0:1]
    for r in range(2):

        def combined(q):
            value = proj[(2 * q + r) * pairs : (2 * q + r + 1) * pairs, :]
            return value[:levels] + sign * value[levels:]

        mask = jnp.where(keep, 1.0, 0.0)[r : r + 1]
        column = local[r] + below[r : r + 1]
        out[0, r] = (combined(0) * mask).astype(jnp.bfloat16)
        second = combined(1) + laplace * (column + combined(2))
        out[1, r] = (second * mask).astype(jnp.bfloat16)
        out[2, r] = (combined(3) * mask).astype(jnp.bfloat16)
    each(band - 1, lambda k: forward(k).wait_send())
    each(band - 1, lambda k: back(k).wait_send())
    each(group - 1, lambda k: across(k).wait_send())


def on_device(
    band, subs, group, spectra, legendre, assignment, circle_longitudes, coriolis, weights,
    thickness,
):
    levels, coeff, lat = spectra.shape[1], spectra.shape[4], legendre.shape[2]
    pairs = 2 * levels
    stride = coeff // band
    block = -(-lat // (128 * band)) * 128
    most = 3 * (band - 1) + 1
    height = -(-most // 8) * 8
    ratio = circle_longitudes // stride
    aliased = (ratio * stride == circle_longitudes) & (ratio < most)
    points = jnp.where(aliased, ratio, most).astype(jnp.float32)
    inverse = 1.0 / points
    rows = jnp.stack(
        [
            points, inverse, circle_longitudes.astype(jnp.float32), coriolis[0], coriolis[1],
            weights[0] * inverse, weights[1] * inverse, jnp.zeros_like(points),
        ]
    )
    rows = jnp.pad(rows, ((0, 0), (0, band * block - lat)))
    sizes = (band, group, subs, stride, levels, coeff, lat, block, most)
    vmem = pl.BlockSpec(memory_space=pltpu.VMEM)
    smem = pl.BlockSpec(memory_space=pltpu.SMEM)
    bf16, f32, dma = jnp.bfloat16, jnp.float32, pltpu.SemaphoreType.DMA
    far, near = max(band - 1, 1), max(group - 1, 1)
    result = pl.pallas_call(
        functools.partial(kernel, sizes),
        out_shape=jax.ShapeDtypeStruct((3, 2, levels, coeff), bf16),
        in_specs=[vmem, pl.BlockSpec(memory_space=pl.ANY), smem, smem, vmem],
        out_specs=vmem,
        scratch_shapes=[
            pltpu.VMEM((coeff, band * block), bf16),
            pltpu.VMEM((6 * pairs, coeff), f32),
            pltpu.VMEM((far, 6 * pairs, block), bf16),
            pltpu.VMEM((band, 6 * pairs, block), bf16),
            pltpu.VMEM((band, height, block), f32),
            pltpu.VMEM((band, height, block), f32),
            pltpu.VMEM((band, 6 * pairs, block), f32),
            pltpu.VMEM((band, 8 * pairs, block), f32),
            pltpu.VMEM((far, 8 * pairs, block), bf16),
            pltpu.VMEM((band, 8 * pairs, block), bf16),
            pltpu.VMEM((8 * pairs, coeff), f32),
            pltpu.VMEM((2, levels, coeff), f32),
            pltpu.VMEM((2, coeff), f32),
            pltpu.VMEM((group, 2, coeff), f32),
            dma,
            dma((far,)),
            dma((far,)),
            dma((far,)),
            dma((far,)),
            dma((near,)),
            dma((near,)),
        ],
        compiler_params=pltpu.CompilerParams(
            collective_id=0, has_side_effects=True, vmem_limit_bytes=48 << 20
        ),
    )(spectra, legendre, assignment, thickness, rows)
    return jnp.transpose(result, (2, 0, 1, 3))[None]


def solution(mesh):
    in_specs = (
        P(("member", "band"), ("fld", "sub"), None, None, None),
        P("band", None, None),
        P(),
        P(),
        P(),
        P(),
        P(("fld", "sub")),
    )
    out_specs = P(("member", "band"), ("fld", "sub"), None, None, None)
    subs = mesh.shape["sub"]
    part = functools.partial(on_device, mesh.shape["band"], subs, subs * mesh.shape["fld"])
    return jax.shard_map(
        part, mesh=mesh, in_specs=in_specs, out_specs=out_specs, check_vma=False
    )
```

time: 40.9 us -> 25.7 us (0.63)
  Pallas kernels: 0 us -> 17.3 us
  starting transfers between devices: 11.4 us -> 0 us
  other arithmetic: 11.5 us -> 1.42 us
  blocking collectives: 5.2 us -> 0 us
  matrix products: 2.53 us -> 0 us
  local copies, waits for them, and re-layouts: 7.92 us -> 6.34 us
  between operations: 0.97 us -> 0.08 us
  waiting for transfers between devices: 0.71 us -> 0 us
    pallas_call x0 -> x1, Pallas kernels: none -> 17.3 us  [on_device(): pl.pallas_call(functools.partial(kernel, sizes), out_shape=jax.ShapeDtype...]
    all_to_all x2 -> x0, starting transfers between devices: 11.4 us -> none  [the longest x1 6.33 us: on_device(): lax.all_to_all(outgoing, 'band', split_axis=0, concat_axis=0, tiled=True)]
    all_gather x1 -> x0, blocking collectives: 5.2 us -> none  [on_device(): sums = lax.all_gather(partial[0], ('fld', 'sub'))]
    unnamed x24 -> x8, local copies, waits for them, and re-layouts: 0.62 us -> 4.06 us
    another operation x6 -> x0, other arithmetic: 3.16 us -> none  [the longest x3 2.48 us: on_device(): jnp.stack([ordered, ordered * parity.astype(jnp.bfloat16)], axis=2)]
    dot_general x2 -> x0, matrix products: 2.53 us -> none  [the longest x1 1.35 us: on_device(): fourier = jnp.dot(stacked, legendre[0], preferred_element_type=jnp.float32)]
    dynamic_slice x2 -> x0, local copies, waits for them, and re-layouts: 2.17 us -> none  [the longest x1 1.39 us: on_device(): own_wave = stride * lax.dynamic_slice_in_dim(assignment, band_place, 1)[0]]
    select_n x5 -> x0, other arithmetic: 2.09 us -> none  [the longest x1 1.41 us: on_device(): jnp.where(live, jnp.cos(angles), 0.0)]
  transfers between devices with their start and end apart: 2 -> 0, of which waited for: 1 -> 0; matrix products, arithmetic and copies ran while one was open for 18% -> 0% of each run, Pallas kernels for 0% -> 0%
where the time goes in v2:
time: 25.7 us; the launch traced here: 25.1 us
  Pallas kernels  17.3 us (67%)
  local copies, waits for them, and re-layouts  6.34 us (25%)
  other arithmetic  1.42 us (6%)
    pallas_call x1, Pallas kernels, on_device(): pl.pallas_call(functools.partial(kernel, sizes), out_shape=jax.ShapeDtype...  17.3 us
    unnamed x8, local copies, waits for them, and re-layouts  4.06 us
    slice x1, local copies, waits for them, and re-layouts, on_device(): weights[1] * inverse  0.81 us
    another operation x7, local copies, waits for them, and re-layouts, on_device(): jnp.stack([points, inverse, circle_longitudes.astype(jnp.float32), coriol...  0.8 us
    mul x1, other arithmetic, on_device(): weights[1] * inverse  0.72 us
    convert_element_type x1, other arithmetic, on_device(): circle_longitudes.astype(jnp.float32)  0.7 us
    broadcast_in_dim x1, local copies, waits for them, and re-layouts, on_device(): return jnp.transpose(result, (2, 0, 1, 3))[None]  0.67 us

profile of v2, /device:TPU:0, one launch (start us, length us, event | category | flops | bytes accessed | tf_op | source)
XLA Modules:
  0.0 25.1 jit_solution(16658806658014416932)
XLA Ops:
  0.0 0.7 %convert_element_type.9 = f32[1280]{0:T(1024)S(1)} convert(s32[1280]{0:T(1024)} %param.10) | non-fusion elementwise | flops 1280 | bytes 10240 | tf_op jit(solution)/shard_map/convert_element_type | solution.py:269
  0.7 0.8 %slice_reduce_fusion = (f32[1280]{0:T(1024)S(1)}, f32[1280]{0:T(1024)S(1)}) fusion(f32[2,1280]{1,0:T(2,128)} %param.12), kind=kLoop, calls=%fused_computation.7 | loop fusion | bytes 20480 | tf_op jit(solution)/shard_map/slice | solution.py:270
  1.5 0.7 %fusion.2 = (f32[1280]{0:T(1024)S(1)}, f32[1280]{0:T(1024)S(1)}) fusion(f32[1280]{0:T(1024)S(1)} %get-tuple-element.5, s32[1280]{0:T(1024)} %param.10), kind=kLoop, calls=%fused_computation.10 | loop fusion | flops 20480 | bytes 20480 | tf_op jit(solution)/shard_map/mul | solution.py:270
  2.3 0.8 %stack.24 = f32[8,1280]{1,0:T(8,128)S(1)} concatenate(f32[1,1280]{1,0:T(1,128)S(1)} %stack.19, f32[1,1280]{1,0:T(1,128)S(1)} %stack.20, f32[1,1280]{1,0:T(1,128)S(1)} %stack.21, f32[2,1280]{1,0:T(2,128)} %param.11, f32[1,1280]{1,0:T(1,128)S(1)} %stack.22, f32[1,1280]{1,0:T(1,128)S(1)} %stack.23, f32[1,1280]{1,0:T(1,128)S(1)} %stack_broadcast_in_dim.3), dimensions={0} | concatenate | bytes 81920 | tf_op jit(solution)/shard_map/stack | solution.py:267
  3.1 0.0 copy-start
  3.1 1.9 %copy-done = bf16[1,1280,1280]{2,1,0:T(8,128)(2,1)S(1)} copy-done((bf16[1,1280,1280]{2,1,0:T(8,128)(2,1)S(1)}, bf16[1,1280,1280]{2,1,0:T(8,128)(2,1)}, u32[]{:S(2)}) %copy-start) | copy-done | bytes 3276824
  5.0 0.0 copy-start.1
  5.0 0.8 %copy-done.1 = bf16[1,4,3,2,1280]{4,3,2,1,0:T(2,128)(2,1)S(1)} copy-done((bf16[1,4,3,2,1280]{4,3,2,1,0:T(2,128)(2,1)S(1)}, bf16[1,4,3,2,1280]{4,3,2,1,0:T(2,128)(2,1)}, u32[]{:S(2)}) %copy-start.1) | copy-done | bytes 61464
  5.9 0.0 copy-start.2
  5.9 0.7 %copy-done.2 = s32[4]{0:T(128)S(1)} copy-done((s32[4]{0:T(128)S(1)}, s32[4]{0:T(128)}, u32[]{:S(2)}) %copy-start.2) | copy-done | bytes 40
  6.5 0.0 copy-start.3
  6.5 0.7 %copy-done.3 = f32[4]{0:T(128)S(1)} copy-done((f32[4]{0:T(128)S(1)}, f32[4]{0:T(128)}, u32[]{:S(2)}) %copy-start.3) | copy-done | bytes 40
  7.2 17.3 %shard_map.73 = bf16[3,2,4,1280]{3,2,1,0:T(4,128)(2,1)S(1)} custom-call(bf16[1,4,3,2,1280]{4,3,2,1,0:T(2,128)(2,1)S(1)} %copy-done.1, bf16[1,1280,1280]{2,1,0:T(8,128)(2,1)S(1)} %copy-done, s32[4]{0:T(128)S(1)} %copy-done.2, f32[4]{0:T(128)S(1)} %copy-done.3, f32[8,1536]{1,0:T(8,128)S(1)} %pad.4.rows), custom_call_target="tpu_custom_call" | custom-call | tf_op jit(solution)/shard_map/pallas_call | solution.py:279
  24.5 0.7 %copy.8 = bf16[1,4,3,2,1280]{4,3,2,1,0:T(2,128)(2,1)} copy(bf16[1,4,3,2,1280]{4,1,3,2,0:T(4,128)(2,1)S(1)} %bitcast.3) | data formatting | bytes 122880 | tf_op jit(solution)/shard_map/broadcast_in_dim | solution.py:311
  (8 shorter events, 0.0 us)
Async XLA Ops:
  3.1 1.9 %copy-start = (bf16[1,1280,1280]{2,1,0:T(8,128)(2,1)S(1)}, bf16[1,1280,1280]{2,1,0:T(8,128)(2,1)}, u32[]{:S(2)}) copy-start(bf16[1,1280,1280]{2,1,0:T(8,128)(2,1)} %legendre.1) | copy-start | bytes 9830404
  5.0 0.8 %copy-start.1 = (bf16[1,4,3,2,1280]{4,3,2,1,0:T(2,128)(2,1)S(1)}, bf16[1,4,3,2,1280]{4,3,2,1,0:T(2,128)(2,1)}, u32[]{:S(2)}) copy-start(bf16[1,4,3,2,1280]{4,3,2,1,0:T(2,128)(2,1)} %spectra.1) | copy-start | bytes 184324
  5.9 0.7 %copy-start.2 = (s32[4]{0:T(128)S(1)}, s32[4]{0:T(128)}, u32[]{:S(2)}) copy-start(s32[4]{0:T(128)} %assignment.1) | copy-start | bytes 52
  6.5 0.7 %copy-start.3 = (f32[4]{0:T(128)S(1)}, f32[4]{0:T(128)}, u32[]{:S(2)}) copy-start(f32[4]{0:T(128)} %thickness.1) | copy-start | bytes 52

commit v3 on v2

v3 whole, which is shorter than its diff:
```python
import functools

import jax
import jax.numpy as jnp
from jax import lax
from jax.experimental import pallas as pl
from jax.experimental.pallas import tpu as pltpu
from jax.sharding import PartitionSpec as P

MESH = pl.DeviceIdType.MESH
COS_TERMS = (1.0, -1 / 2, 1 / 24, -1 / 720, 1 / 40320, -1 / 3628800, 1 / 479001600)
SIN_TERMS = (1.0, -1 / 6, 1 / 120, -1 / 5040, 1 / 362880, -1 / 39916800, 1 / 6227020800)
PI = 3.141592653589793


def each(count, body):
    if count <= 8:
        for i in range(count):
            body(i)
    else:

        def step(i, carry):
            body(i)
            return carry

        lax.fori_loop(0, count, step, 0)


def series(terms, square):
    value = jnp.full_like(square, terms[-1])
    for term in terms[-2::-1]:
        value = value * square + term
    return value


def circle(turns):
    half = PI * turns
    square = half * half
    sine = half * series(SIN_TERMS, square)
    cosine = series(COS_TERMS, square)
    return 1.0 - 2.0 * sine * sine, 2.0 * sine * cosine


def kernel(
    sizes, spectra_far, legendre, assignment_far, circles_far, coriolis_far, weights_far,
    thickness_far, out, table, spectra, assignment, circles, coriolis, weights, thickness,
    wide, fsend, frecv, costab, sintab, coeffs, sums, bsend, brecv, proj, local, colsend, colrecv,
    load_sem, small_sem, fs_sem, fr_sem, bs_sem, br_sem, cs_sem, cr_sem,
):
    band, group, subs, stride, levels, coeff, lat, least, first_wide, last_wide, most = sizes
    pairs = 2 * levels
    widest = min(least + first_wide + last_wide, least + 1)
    block = 128 * widest
    me = lax.axis_index("band")
    mine = lax.axis_index("fld") * subs + lax.axis_index("sub")

    def width(b):
        wide_one = (b < first_wide) | (b >= band - last_wide)
        return jnp.where(wide_one, widest, least)

    def lanes(b):
        tile = b * least + jnp.minimum(b, first_wide) + jnp.maximum(b - (band - last_wide), 0)
        return pl.ds(pl.multiple_of(tile * 128, 128), block)

    def tiles(b, body):
        for c in range(widest):
            if c < least:
                body(c)
            else:
                pl.when(width(b) > c)(functools.partial(body, c))

    def tile(c):
        return pl.ds(128 * c, 128)

    def band_peer(k):
        return {"band": lax.rem(me + k, band)}

    def group_peer(k):
        peer = lax.rem(mine + k, group)
        return {"fld": peer // subs, "sub": lax.rem(peer, subs)}

    pairs_of = (
        (spectra_far, spectra), (assignment_far, assignment), (circles_far, circles),
        (coriolis_far, coriolis), (weights_far, weights), (thickness_far, thickness),
    )
    small = [
        pltpu.make_async_copy(far, near, small_sem.at[i]) for i, (far, near) in enumerate(pairs_of)
    ]
    load = pltpu.make_async_copy(legendre.at[0], table, load_sem)
    for copy in small:
        copy.start()
    load.start()
    if widest > least:
        frecv[:, :, 128 * least :] = jnp.zeros((band, 6 * pairs, 128), jnp.bfloat16)
        brecv[:, :, 128 * least :] = jnp.zeros((band, 8 * pairs, 128), jnp.bfloat16)
    barrier = pltpu.get_barrier_semaphore()

    def greet_band(k):
        pl.semaphore_signal(barrier, inc=1, device_id=band_peer(k + 1), device_id_type=MESH)

    def greet_group(k):
        pl.semaphore_signal(barrier, inc=1, device_id=group_peer(k + 1), device_id_type=MESH)

    each(band - 1, greet_band)
    each(group - 1, greet_group)
    for copy in small:
        copy.wait()

    own = stride * assignment[me]
    index = lax.broadcasted_iota(jnp.int32, (2, coeff), 1)
    part = lax.broadcasted_iota(jnp.int32, (2, coeff), 0)
    keep = (index < coeff - own) & (part * jnp.where(own == 0, 1, 0) == 0)
    parity = (1 - 2 * lax.rem(index, 2)).astype(jnp.float32)
    for level in range(levels):
        for field in range(3):
            value = jnp.where(keep, spectra[0, level, field].astype(jnp.float32), 0.0)
            other = value * parity
            for r in range(2):
                row = (2 * field + r) * pairs + level
                wide[row : row + 1, :] = value[r : r + 1]
                wide[row + levels : row + levels + 1, :] = other[r : r + 1]
    both = wide[...].astype(jnp.bfloat16)

    def forward(k, c):
        return pltpu.make_async_remote_copy(
            src_ref=fsend.at[k, :, tile(c)], dst_ref=frecv.at[me, :, tile(c)],
            send_sem=fs_sem.at[k, c], recv_sem=fr_sem.at[k, c], device_id=band_peer(k + 1),
            device_id_type=MESH,
        )

    def back(k, c):
        return pltpu.make_async_remote_copy(
            src_ref=bsend.at[k, :, tile(c)], dst_ref=brecv.at[me, :, tile(c)],
            send_sem=bs_sem.at[k, c], recv_sem=br_sem.at[k, c], device_id=band_peer(k + 1),
            device_id_type=MESH,
        )

    def across(k):
        return pltpu.make_async_remote_copy(
            src_ref=colsend, dst_ref=colrecv.at[mine], send_sem=cs_sem.at[k],
            recv_sem=cr_sem.at[k], device_id=group_peer(k + 1), device_id_type=MESH,
        )

    load.wait()
    pl.semaphore_wait(barrier, band + group - 2)

    def transform(b):
        return jnp.dot(both, table[:, lanes(b)], preferred_element_type=jnp.float32).astype(
            jnp.bfloat16
        )

    def send_forward(k):
        b = lax.rem(me + k + 1, band)
        fsend[k] = transform(b)
        tiles(b, lambda c: forward(k, c).start())

    each(band - 1, send_forward)
    frecv[me] = transform(me)

    for r in range(2):
        total = None
        for level in range(levels - 1, -1, -1):
            row = (4 + r) * pairs + level
            value = thickness[level] * wide[row : row + 1, :]
            total = value if total is None else total + value
            local[r, level : level + 1, :] = total
        colsend[r : r + 1, :] = total
    each(group - 1, lambda k: across(k).start())

    counts = circles[lanes(me)].astype(jnp.float32).reshape(1, block)
    ratio = jnp.floor(counts * (1.0 / stride) + 0.5)
    points = jnp.where((ratio * stride == counts) & (ratio < most), ratio, float(most))
    inverse = 1.0 / points
    height = costab.shape[2]
    xs = lax.broadcasted_iota(jnp.int32, (height, block), 0).astype(jnp.float32)
    pair = lax.broadcasted_iota(jnp.int32, (pairs, block), 0)
    lane = lax.broadcasted_iota(jnp.int32, (pairs, block), 1)
    north, south = coriolis[0:1, lanes(me)], coriolis[1:2, lanes(me)]
    spin = jnp.where(pair < levels, north, south)
    north, south = weights[0:1, lanes(me)], weights[1:2, lanes(me)]
    quad = jnp.where(pair < levels, north, south) * inverse
    quad = jnp.where(lane < 128 * width(me), quad, 0.0)

    def fill(s):
        phase = xs * assignment[s].astype(jnp.float32)
        phase = phase - points * jnp.floor(phase * inverse)
        turns = phase * inverse
        cosine, sine = circle(turns - jnp.floor(turns + 0.5))
        cosine = jnp.where(xs < points, cosine, 0.0)
        sine = jnp.where(xs < points, sine, 0.0)
        for c in range(widest):
            costab[s, c] = cosine[:, 128 * c : 128 * c + 128]
            sintab[s, c] = sine[:, 128 * c : 128 * c + 128]

    each(band, fill)

    def sample(c):
        here = slice(128 * c, 128 * c + 128)
        number = counts[:, here]

        def twice(s):
            return 2.0 * (stride * assignment[s]).astype(jnp.float32)

        def weigh(s):
            double = twice(s)
            gain = jnp.where(double < number, jnp.where(double == 0.0, 1.0, 2.0), 0.0)
            coeffs[s] = frecv[s, :, here].astype(jnp.float32) * gain

        def add_wave(x, s, fields):
            cosine = costab[s, c, pl.ds(x, 1), :]
            sine = sintab[s, c, pl.ds(x, 1), :]
            return tuple(
                fields[f]
                + coeffs[s, 2 * f * pairs : (2 * f + 1) * pairs, :] * cosine
                - coeffs[s, (2 * f + 1) * pairs : (2 * f + 2) * pairs, :] * sine
                for f in range(3)
            )

        def products(fields):
            vort, div, theta = fields
            absolute = vort + spin[:, here]
            return (
                -absolute * div,
                absolute * vort,
                0.5 * (vort * vort + div * div),
                -theta * div,
            )

        nothing = jnp.zeros((pairs, 128), jnp.float32)

        def scaled(s, q, value):
            scale = jnp.where(twice(s) < number, quad[:, here], 0.0)
            sums[s, q * pairs : (q + 1) * pairs, here] = value * scale

        each(band, weigh)
        if band <= 4:

            def point(x, totals):
                fields = (nothing,) * 3
                for s in range(band):
                    fields = add_wave(x, s, fields)
                terms = products(fields)
                result = []
                for s in range(band):
                    cosine = costab[s, c, pl.ds(x, 1), :]
                    sine = sintab[s, c, pl.ds(x, 1), :]
                    for q in range(4):
                        result.append(totals[8 * s + 2 * q] + terms[q] * cosine)
                        result.append(totals[8 * s + 2 * q + 1] - terms[q] * sine)
                return tuple(result)

            totals = lax.fori_loop(0, most, point, (nothing,) * (8 * band))
            for s in range(band):
                for q in range(8):
                    scaled(s, q, totals[8 * s + q])
        else:

            def clear(s):
                sums[s, :, here] = jnp.zeros((8 * pairs, 128), jnp.float32)

            def point(x, carry):
                fields = lax.fori_loop(
                    0, band, functools.partial(add_wave, x), (nothing,) * 3
                )
                terms = products(fields)

                def collect(s):
                    cosine = costab[s, c, pl.ds(x, 1), :]
                    sine = sintab[s, c, pl.ds(x, 1), :]
                    for q in range(4):
                        real = slice(2 * q * pairs, (2 * q + 1) * pairs)
                        imag = slice((2 * q + 1) * pairs, (2 * q + 2) * pairs)
                        sums[s, real, here] += terms[q] * cosine
                        sums[s, imag, here] -= terms[q] * sine

                each(band, collect)
                return carry

            def settle(s):
                for q in range(8):
                    scaled(s, q, sums[s, q * pairs : (q + 1) * pairs, here])

            each(band, clear)
            lax.fori_loop(0, most, point, 0)
            each(band, settle)

        def send_back(k):
            value = sums[lax.rem(me + k + 1, band), :, here]
            bsend[k, :, here] = value.astype(jnp.bfloat16)
            back(k, c).start()

        each(band - 1, send_back)
        brecv[me, :, here] = sums[me, :, here].astype(jnp.bfloat16)

    def arrive(c):
        each(band - 1, lambda k: forward(k, c).wait_recv())
        sample(c)

    tiles(me, arrive)

    def project(b):
        return lax.dot_general(
            brecv[b], table[:, lanes(b)], (((1,), (1,)), ((), ())),
            preferred_element_type=jnp.float32,
        )

    proj[...] = project(me)

    def gather_back(k):
        b = lax.rem(me + band - k - 1, band)
        tiles(b, lambda c: back(k, c).wait_recv())
        proj[...] += project(b)

    each(band - 1, gather_back)
    each(group - 1, lambda k: across(k).wait_recv())
    below = jnp.zeros((2, coeff), jnp.float32)
    for k in range(group - 1):
        sender = lax.rem(mine + group - k - 1, group)
        below = below + jnp.where(sender > mine, 1.0, 0.0) * colrecv[sender]
    degree = own + index[0:1]
    laplace = (degree * (degree + 1)).astype(jnp.float32) * (1.0 / float((coeff - 1) * coeff))
    sign = parity[0:1]
    for r in range(2):

        def combined(q):
            value = proj[(2 * q + r) * pairs : (2 * q + r + 1) * pairs, :]
            return value[:levels] + sign * value[levels:]

        mask = jnp.where(keep, 1.0, 0.0)[r : r + 1]
        column = local[r] + below[r : r + 1]
        out[0, r] = (combined(0) * mask).astype(jnp.bfloat16)
        second = combined(1) + laplace * (column + combined(2))
        out[1, r] = (second * mask).astype(jnp.bfloat16)
        out[2, r] = (combined(3) * mask).astype(jnp.bfloat16)

    def sent(k):
        tiles(lax.rem(me + k + 1, band), lambda c: forward(k, c).wait_send())
        tiles(me, lambda c: back(k, c).wait_send())

    each(band - 1, sent)
    each(group - 1, lambda k: across(k).wait_send())


def on_device(
    band, subs, group, spectra, legendre, assignment, circle_longitudes, coriolis, weights,
    thickness,
):
    levels, coeff, lat = spectra.shape[1], spectra.shape[4], legendre.shape[2]
    pairs = 2 * levels
    stride = coeff // band
    least, extra = divmod(lat // 128, band)
    last_wide = -(-extra // 2)
    block = 128 * (least + (1 if extra else 0))
    most = 3 * (band - 1) + 1
    height = -(-most // 8) * 8
    sizes = (
        band, group, subs, stride, levels, coeff, lat, least, extra - last_wide, last_wide, most,
    )
    far_away = pl.BlockSpec(memory_space=pltpu.MemorySpace.HBM)
    bf16, f32, dma = jnp.bfloat16, jnp.float32, pltpu.SemaphoreType.DMA
    far, near, many = max(band - 1, 1), max(group - 1, 1), block // 128
    result = pl.pallas_call(
        functools.partial(kernel, sizes),
        out_shape=jax.ShapeDtypeStruct((3, 2, levels, coeff), bf16),
        in_specs=[far_away] * 7,
        out_specs=pl.BlockSpec(memory_space=pltpu.VMEM),
        scratch_shapes=[
            pltpu.VMEM((coeff, lat), bf16),
            pltpu.VMEM(spectra.shape, bf16),
            pltpu.SMEM((band,), jnp.int32),
            pltpu.VMEM((lat,), jnp.int32),
            pltpu.VMEM((2, lat), f32),
            pltpu.VMEM((2, lat), f32),
            pltpu.SMEM((levels,), f32),
            pltpu.VMEM((6 * pairs, coeff), f32),
            pltpu.VMEM((far, 6 * pairs, block), bf16),
            pltpu.VMEM((band, 6 * pairs, block), bf16),
            pltpu.VMEM((band, many, height, 128), f32),
            pltpu.VMEM((band, many, height, 128), f32),
            pltpu.VMEM((band, 6 * pairs, 128), f32),
            pltpu.VMEM((band, 8 * pairs, block), f32),
            pltpu.VMEM((far, 8 * pairs, block), bf16),
            pltpu.VMEM((band, 8 * pairs, block), bf16),
            pltpu.VMEM((8 * pairs, coeff), f32),
            pltpu.VMEM((2, levels, coeff), f32),
            pltpu.VMEM((2, coeff), f32),
            pltpu.VMEM((group, 2, coeff), f32),
            dma,
            dma((6,)),
            dma((far, many)),
            dma((far, many)),
            dma((far, many)),
            dma((far, many)),
            dma((near,)),
            dma((near,)),
        ],
        compiler_params=pltpu.CompilerParams(
            collective_id=0, has_side_effects=True, vmem_limit_bytes=64 << 20
        ),
    )(
        spectra, legendre, assignment, circle_longitudes, coriolis, weights, thickness,
    )
    return jnp.transpose(result, (2, 0, 1, 3))[None]


def solution(mesh):
    in_specs = (
        P(("member", "band"), ("fld", "sub"), None, None, None),
        P("band", None, None),
        P(),
        P(),
        P(),
        P(),
        P(("fld", "sub")),
    )
    out_specs = P(("member", "band"), ("fld", "sub"), None, None, None)
    subs = mesh.shape["sub"]
    part = functools.partial(on_device, mesh.shape["band"], subs, subs * mesh.shape["fld"])
    return jax.shard_map(
        part, mesh=mesh, in_specs=in_specs, out_specs=out_specs, check_vma=False
    )
```

time: 25.7 us -> 18.7 us (0.73); the launches traced: 25.1 us -> 18.5 us
  local copies, waits for them, and re-layouts: 6.34 us -> 1.5 us
  other arithmetic: 1.42 us -> 0 us
  Pallas kernels: 17.3 us -> 17 us
    unnamed x8 -> x0, local copies, waits for them, and re-layouts: 4.06 us -> none
    broadcast_in_dim x1, local copies, waits for them, and re-layouts: 0.67 us -> 1.5 us  [on_device(): return jnp.transpose(result, (2, 0, 1, 3))[None]]
    slice x1 -> x0, local copies, waits for them, and re-layouts: 0.81 us -> none  [on_device(): weights[1] * inverse]
    another operation x7 -> x0, local copies, waits for them, and re-layouts: 0.8 us -> none  [on_device(): jnp.stack([points, inverse, circle_longitudes.astype(jnp.float32), coriol...]
    mul x2 -> x0, other arithmetic: 0.72 us -> none  [the longest x1 0.72 us: on_device(): weights[1] * inverse]
    convert_element_type x1 -> x0, other arithmetic: 0.7 us -> none  [on_device(): circle_longitudes.astype(jnp.float32)]
    pallas_call x1, Pallas kernels: 17.3 us -> 17 us  [on_device(): pl.pallas_call(functools.partial(kernel, sizes), out_shape=jax.ShapeDtype...]
where the time goes in v3:
time: 18.7 us; the launch traced here: 18.5 us
  Pallas kernels  17 us (91%)
  local copies, waits for them, and re-layouts  1.5 us (8%)
    pallas_call x1, Pallas kernels, on_device(): pl.pallas_call(functools.partial(kernel, sizes), out_shape=jax.ShapeDtype...  17 us
    broadcast_in_dim x1, local copies, waits for them, and re-layouts, on_device(): return jnp.transpose(result, (2, 0, 1, 3))[None]  1.5 us

profile of v3, /device:TPU:0, one launch (start us, length us, event | category | flops | bytes accessed | tf_op | source)
XLA Modules:
  0.0 18.5 jit_solution(5240370466003708611)
XLA Ops:
  0.0 17.0 %shard_map.73 = bf16[3,2,4,1280]{3,2,1,0:T(4,128)(2,1)} custom-call(bf16[1,4,3,2,1280]{4,3,2,1,0:T(2,128)(2,1)} %spectra_far.1, bf16[1,1280,1280]{2,1,0:T(8,128)(2,1)} %legendre.1, s32[4]{0:T(128)} %assignment_far.1, s32[1280]{0:T(1024)} %circles_far.1, f32[2,1280]{1,0:T(2,128)} %coriolis_far.1, f32[2,1280]{1,0:T(2,128)} %weights_far.1, f32[4]{0:T(128)} %thickness_far.1), custom_call_target="tpu_custom_call" | custom-call | tf_op jit(solution)/shard_map/pallas_call | solution.py:362
  17.0 1.5 %copy.8 = bf16[1,4,3,2,1280]{4,3,2,1,0:T(2,128)(2,1)} copy(bf16[1,4,3,2,1280]{4,1,3,2,0:T(4,128)(2,1)} %bitcast.3) | data formatting | bytes 122880 | tf_op jit(solution)/shard_map/broadcast_in_dim | solution.py:403

commit v4 on v3

--- a/solution.py
+++ b/solution.py
@@ -92,7 +92,6 @@
     load.start()
     if widest > least:
         frecv[:, :, 128 * least :] = jnp.zeros((band, 6 * pairs, 128), jnp.bfloat16)
-        brecv[:, :, 128 * least :] = jnp.zeros((band, 8 * pairs, 128), jnp.bfloat16)
     barrier = pltpu.get_barrier_semaphore()
 
     def greet_band(k):
@@ -152,9 +151,15 @@
     def send_forward(k):
         b = lax.rem(me + k + 1, band)
         fsend[k] = transform(b)
-        tiles(b, lambda c: forward(k, c).start())
+        tiles(b, lambda c: forward(k, c).start() if c == 0 else None)
+
+    def send_rest(wanted, k):
+        b = lax.rem(me + k + 1, band)
+        tiles(b, lambda c: forward(k, c).start() if c == wanted else None)
 
     each(band - 1, send_forward)
+    for c in range(1, widest):
+        each(band - 1, functools.partial(send_rest, c))
     frecv[me] = transform(me)
 
     for r in range(2):
@@ -298,20 +303,43 @@
 
     tiles(me, arrive)
 
-    def project(b):
-        return lax.dot_general(
-            brecv[b], table[:, lanes(b)], (((1,), (1,)), ((), ())),
+    def project(b, start, stop):
+        lane = lanes(b)
+        part = pl.ds(pl.multiple_of(lane.start + start, 128), stop - start)
+        proj[...] += lax.dot_general(
+            brecv[b, :, start:stop], table[:, part], (((1,), (1,)), ((), ())),
             preferred_element_type=jnp.float32,
         )
 
-    proj[...] = project(me)
-
-    def gather_back(k):
+    def extra(b, body):
+        pl.when(width(b) > least)(body)
+
+    proj[...] = jnp.zeros(proj.shape, jnp.float32)
+    inner = 128 * least
+    if least:
+        project(me, 0, inner)
+    if widest > least:
+        extra(me, lambda: project(me, inner, block))
+
+    def gather_even(k):
         b = lax.rem(me + band - k - 1, band)
-        tiles(b, lambda c: back(k, c).wait_recv())
-        proj[...] += project(b)
-
-    each(band - 1, gather_back)
+        for c in range(least):
+            back(k, c).wait_recv()
+        project(b, 0, inner)
+
+    def gather_extra(k):
+        b = lax.rem(me + band - k - 1, band)
+
+        def last():
+            back(k, least).wait_recv()
+            project(b, inner, block)
+
+        extra(b, last)
+
+    if least:
+        each(band - 1, gather_even)
+    if widest > least:
+        each(band - 1, gather_extra)
     each(group - 1, lambda k: across(k).wait_recv())
     below = jnp.zeros((2, coeff), jnp.float32)
     for k in range(group - 1):
@@ -320,6 +348,7 @@
     degree = own + index[0:1]
     laplace = (degree * (degree + 1)).astype(jnp.float32) * (1.0 / float((coeff - 1) * coeff))
     sign = parity[0:1]
+    results = []
     for r in range(2):
 
         def combined(q):
@@ -328,10 +357,12 @@
 
         mask = jnp.where(keep, 1.0, 0.0)[r : r + 1]
         column = local[r] + below[r : r + 1]
-        out[0, r] = (combined(0) * mask).astype(jnp.bfloat16)
         second = combined(1) + laplace * (column + combined(2))
-        out[1, r] = (second * mask).astype(jnp.bfloat16)
-        out[2, r] = (combined(3) * mask).astype(jnp.bfloat16)
+        results.append((combined(0) * mask, second * mask, combined(3) * mask))
+    for level in range(levels):
+        for field in range(3):
+            rows = [results[r][field][level : level + 1] for r in range(2)]
+            out[0, level, field] = jnp.concatenate(rows, axis=0).astype(jnp.bfloat16)
 
     def sent(k):
         tiles(lax.rem(me + k + 1, band), lambda c: forward(k, c).wait_send())
@@ -361,7 +392,7 @@
     far, near, many = max(band - 1, 1), max(group - 1, 1), block // 128
     result = pl.pallas_call(
         functools.partial(kernel, sizes),
-        out_shape=jax.ShapeDtypeStruct((3, 2, levels, coeff), bf16),
+        out_shape=jax.ShapeDtypeStruct(spectra.shape, bf16),
         in_specs=[far_away] * 7,
         out_specs=pl.BlockSpec(memory_space=pltpu.VMEM),
         scratch_shapes=[
@@ -400,7 +431,7 @@
     )(
         spectra, legendre, assignment, circle_longitudes, coriolis, weights, thickness,
     )
-    return jnp.transpose(result, (2, 0, 1, 3))[None]
+    return result
 
 
 def solution(mesh):

time: 18.7 us -> 18.1 us (0.968)
  Pallas kernels: 17 us -> 16.5 us
    broadcast_in_dim x1 -> x0, local copies, waits for them, and re-layouts: 1.5 us -> none  [on_device(): return jnp.transpose(result, (2, 0, 1, 3))[None]]
    unnamed x0 -> x1, local copies, waits for them, and re-layouts: none -> 1.5 us
    pallas_call x1, Pallas kernels: 17 us -> 16.5 us  [on_device(): pl.pallas_call(functools.partial(kernel, sizes), out_shape=jax.ShapeDtype...]
where the time goes in v4:
time: 18.1 us; the launch traced here: 18 us
  Pallas kernels  16.5 us (91%)
  local copies, waits for them, and re-layouts  1.5 us (8%)
    pallas_call x1, Pallas kernels, on_device(): pl.pallas_call(functools.partial(kernel, sizes), out_shape=jax.ShapeDtype...  16.5 us
    unnamed x1, local copies, waits for them, and re-layouts  1.5 us

profile of v4, /device:TPU:0, one launch (start us, length us, event | category | flops | bytes accessed | tf_op | source)
XLA Modules:
  0.0 18.0 jit_solution(15526298656827626082)
XLA Ops:
  0.0 16.5 %shard_map.73 = bf16[1,4,3,2,1280]{4,3,2,1,0:T(2,128)(2,1)} custom-call(bf16[1,4,3,2,1280]{4,3,2,1,0:T(2,128)(2,1)} %spectra_far.1, bf16[1,1280,1280]{2,1,0:T(8,128)(2,1)} %legendre.1, s32[4]{0:T(128)} %assignment_far.1, s32[1280]{0:T(1024)} %circles_far.1, f32[2,1280]{1,0:T(2,128)} %coriolis_far.1, f32[2,1280]{1,0:T(2,128)} %weights_far.1, f32[4]{0:T(128)} %thickness_far.1), custom_call_target="tpu_custom_call" | custom-call | tf_op jit(solution)/shard_map/pallas_call | solution.py:393
  16.5 1.5 %copy.9 = bf16[1,4,3,2,1280]{4,3,2,1,0:T(2,128)(2,1)} copy(bf16[1,4,3,2,1280]{4,3,2,1,0:T(2,128)(2,1)} %shard_map.73) | data formatting | bytes 122880

commit v5 on v4

--- a/solution.py
+++ b/solution.py
@@ -254,7 +254,9 @@
                         result.append(totals[8 * s + 2 * q + 1] - terms[q] * sine)
                 return tuple(result)
 
-            totals = lax.fori_loop(0, most, point, (nothing,) * (8 * band))
+            totals = (nothing,) * (8 * band)
+            for x in range(most):
+                totals = point(x, totals)
             for s in range(band):
                 for q in range(8):
                     scaled(s, q, totals[8 * s + q])
@@ -362,7 +364,7 @@
     for level in range(levels):
         for field in range(3):
             rows = [results[r][field][level : level + 1] for r in range(2)]
-            out[0, level, field] = jnp.concatenate(rows, axis=0).astype(jnp.bfloat16)
+            out[0, level, field] = jnp.concatenate(rows, axis=0)
 
     def sent(k):
         tiles(lax.rem(me + k + 1, band), lambda c: forward(k, c).wait_send())
@@ -392,7 +394,7 @@
     far, near, many = max(band - 1, 1), max(group - 1, 1), block // 128
     result = pl.pallas_call(
         functools.partial(kernel, sizes),
-        out_shape=jax.ShapeDtypeStruct(spectra.shape, bf16),
+        out_shape=jax.ShapeDtypeStruct(spectra.shape, f32),
         in_specs=[far_away] * 7,
         out_specs=pl.BlockSpec(memory_space=pltpu.VMEM),
         scratch_shapes=[
@@ -431,7 +433,7 @@
     )(
         spectra, legendre, assignment, circle_longitudes, coriolis, weights, thickness,
     )
-    return result
+    return result.astype(bf16)
 
 
 def solution(mesh):

time: 18.1 us -> 18.1 us (level)
  other arithmetic: 0 us -> 1.57 us
  local copies, waits for them, and re-layouts: 1.5 us -> 0 us
  Pallas kernels: 16.5 us -> 16.3 us
    convert_element_type x0 -> x1, other arithmetic: none -> 1.57 us  [on_device(): return result.astype(bf16)]
    unnamed x1 -> x0, local copies, waits for them, and re-layouts: 1.5 us -> none
where the time goes in v5:
time: 18.1 us; the launch traced here: 17.9 us
  Pallas kernels  16.3 us (90%)
  other arithmetic  1.57 us (9%)
    pallas_call x1, Pallas kernels, on_device(): pl.pallas_call(functools.partial(kernel, sizes), out_shape=jax.ShapeDtype...  16.3 us
    convert_element_type x1, other arithmetic, on_device(): return result.astype(bf16)  1.57 us

profile of v5, /device:TPU:0, one launch (start us, length us, event | category | flops | bytes accessed | tf_op | source)
XLA Modules:
  0.0 17.9 jit_solution(9893181260563401201)
XLA Ops:
  0.0 16.3 %shard_map.73 = f32[1,4,3,2,1280]{4,3,2,1,0:T(2,128)} custom-call(bf16[1,4,3,2,1280]{4,3,2,1,0:T(2,128)(2,1)} %spectra_far.1, bf16[1,1280,1280]{2,1,0:T(8,128)(2,1)} %legendre.1, s32[4]{0:T(128)} %assignment_far.1, s32[1280]{0:T(1024)} %circles_far.1, f32[2,1280]{1,0:T(2,128)} %coriolis_far.1, f32[2,1280]{1,0:T(2,128)} %weights_far.1, f32[4]{0:T(128)} %thickness_far.1), custom_call_target="tpu_custom_call" | custom-call | tf_op jit(solution)/shard_map/pallas_call | solution.py:395
  16.3 1.6 %convert_element_type.3 = bf16[1,4,3,2,1280]{4,3,2,1,0:T(2,128)(2,1)} convert(f32[1,4,3,2,1280]{4,3,2,1,0:T(2,128)} %shard_map.73) | non-fusion elementwise | flops 30720 | bytes 184320 | tf_op jit(solution)/shard_map/convert_element_type | solution.py:436
